TPU v7x, 256 devices: a whole 4x4x8 slice. The times are simulated.
256 devices in a mesh: fsdp: 16 (over y, z_hi, core), tp: 16 (over x, z_lo).
Axes of the slice: x: 4, y: 4, z: 8 (z_hi: 2, z_lo: 4; z = z_hi * 4 + z_lo), core: 2. Of those that a mesh axis runs over, the one named last changes fastest.
Arguments:
- tokens: bfloat16 [16384, 4096], P(('fsdp', 'tp')), may hold values from -6 to 6
- norm_gain: float32 [4096], replicated, may hold values from 0.5 to 2
- up_blocks: bfloat16 [256, 24, 64, 64], P(('tp', 'fsdp')), may hold values from -0.1875 to 0.1875
- up_rows: int32 [256, 24], P(('tp', 'fsdp')), may hold values from 0 to 63, as said below
- up_count: int32 [256], P(('tp', 'fsdp')), may hold values from 12 to 24, as said below
- down_blocks: bfloat16 [16, 64, 6, 64, 64], P('tp', 'fsdp'), may hold values from -0.09375 to 0.09375
- down_rows: int32 [16, 64, 6], P('tp', 'fsdp'), may hold values from 0 to 15, as said below
- down_count: int32 [16, 64], P('tp', 'fsdp'), may hold values from 3 to 6, as said below
Outputs:
- mixed: bfloat16 [16384, 4096], P(('fsdp', 'tp'))
Inputs may be any that keep to these rules, and one draw needn't show every extreme that they name: `up_rows`: the slots of one hidden block column name distinct input blocks. `up_count`: some hidden block column has exactly 24 live slots. `down_rows`: the slots of one panel and output block column name distinct hidden blocks of that panel. `down_count`: some panel and output block column has exactly 6 live slots.
All inputs are finite; a program needn't handle non-finite values.
Results may differ from a plain program's by a relative error of at most 0.014.
Values may be sent and summed in bfloat16 or wider, within the bound.
A program may use at most 128 MiB of HBM per device.

v0:
```python
import jax
import jax.numpy as jnp
from jax import lax
from jax.sharding import PartitionSpec as P

D = 4096
FF = 16384
BLK = 64


def dense_weights(weights, rows, count, span):
    columns, slots, side, _ = weights.shape
    slot_ids = jnp.arange(slots, dtype=jnp.int32)
    block_ids = jnp.arange(span, dtype=jnp.int32)
    live = slot_ids[None, :] < count[:, None]
    onehot = ((rows[:, :, None] == block_ids[None, None, :]) & live[:, :, None]).astype(
        jnp.bfloat16
    )
    dense = jnp.einsum("csb,cskn->bkcn", onehot, weights, preferred_element_type=jnp.float32)
    return dense.astype(jnp.bfloat16).reshape(span * side, columns * side)


def sparse_up(row_blocks, weights, rows, count):
    slot_ids = jnp.arange(weights.shape[1], dtype=jnp.int32)

    def one_column(packed):
        column_w, column_r, column_c = packed
        live = (slot_ids < column_c).astype(jnp.bfloat16)
        masked = column_w * live[:, None, None]
        picked = jnp.take(row_blocks, column_r, axis=1)
        return jnp.einsum("tsk,skn->tn", picked, masked, preferred_element_type=jnp.float32)

    stacked = lax.map(one_column, (weights, rows, count))
    columns, total_rows, side = stacked.shape
    return jnp.transpose(stacked, (1, 0, 2)).reshape(total_rows, columns * side)


def on_device(tokens, norm_gain, up_blocks, up_rows, up_count, down_blocks, down_rows, down_count):
    x_float = tokens.astype(jnp.float32)
    scale = lax.rsqrt(jnp.mean(x_float * x_float, axis=-1, keepdims=True) + 1e-05)
    normed = (x_float * scale * norm_gain).astype(jnp.bfloat16)
    gathered = lax.all_gather(normed, "tp", axis=0, tiled=True)
    row_blocks = gathered.reshape(gathered.shape[0], D // BLK, BLK)
    local_down = (down_blocks[0], down_rows[0], down_count[0])
    panel_span = FF // BLK // lax.axis_size("tp")
    piece = lax.all_gather((up_blocks, up_rows, up_count), "fsdp", axis=0, tiled=True)
    pre = sparse_up(row_blocks, piece[0], piece[1], piece[2])
    hidden = jax.nn.gelu(pre, approximate=True).astype(jnp.bfloat16)
    piece = lax.all_gather(
        (local_down[0], local_down[1], local_down[2]), "fsdp", axis=0, tiled=True
    )
    partial_sums = jnp.dot(
        hidden,
        dense_weights(piece[0], piece[1], piece[2], panel_span),
        preferred_element_type=jnp.float32,
    )
    summed = lax.psum_scatter(
        partial_sums.astype(jnp.bfloat16), "tp", scatter_dimension=0, tiled=True
    ).astype(jnp.float32)
    return (x_float + summed).astype(jnp.bfloat16)


def solution(mesh):
    placed = (
        P(("fsdp", "tp"), None),
        P(),
        P(("tp", "fsdp"), None, None, None),
        P(("tp", "fsdp"), None),
        P(("tp", "fsdp")),
        P("tp", "fsdp", None, None, None),
        P("tp", "fsdp", None),
        P("tp", "fsdp"),
    )
    return jax.shard_map(
        on_device, mesh=mesh, in_specs=placed, out_specs=P(("fsdp", "tp"), None), check_vma=False
    )
```

profile of v0, /device:TPU:1, one launch (start us, length us, event | category | flops | bytes accessed | tf_op | source)
XLA Modules:
  0.0 752.0 jit_solution(16629910633116530756)
XLA Ops:
  15.6 17.4 %all-reduce.2 = (s32[16]{0:T(128)}, s32[64]{0:T(128)S(1)}) all-reduce(s32[16]{0:T(128)S(1)} %dynamic-update-slice, s32[64]{0:T(128)S(1)} %bitcast_dynamic-update-slice_fusion), channel_id=1, replica_groups=mesh['fsdp'=16,'tp'=16] {'fsdp'}, use_global_device_ids=true, to_apply=%add | all-reduce | flops 80 | bytes 640
  33.0 31.4 %all-gather.3 = s32[16,1,24]{2,1,0:T(1,128)S(1)} all-gather(s32[1,1,24]{2,1,0:T(1,128)} %bitcast.67), channel_id=1, replica_groups=mesh['fsdp'=16,'tp'=16] {'fsdp'}, dimensions={0}, use_global_device_ids=true | all-gather | bytes 1632 | tf_op jit(solution)/shard_map/all_gather | solution.py:46
  64.4 28.0 %all-gather = s32[1,64,6]{2,0,1:T(1,128)S(1)} all-gather(s32[1,4,6]{2,0,1:T(1,128)} %bitcast.66), channel_id=2, replica_groups=mesh['fsdp'=16,'tp'=16] {'fsdp'}, dimensions={1}, use_global_device_ids=true | all-gather | bytes 1632 | tf_op jit(solution)/shard_map/all_gather | solution.py:49
  92.5 15.0 %all-gather.12.cloned.1.call-done = bf16[1,64,6,64,64]{4,3,2,0,1:T(8,128)(2,1)} async-done(((bf16[1,4,6,64,64]{4,3,2,0,1:T(8,128)(2,1)}), bf16[1,64,6,64,64]{4,3,2,0,1:T(8,128)(2,1)}) %all-gather.12.cloned.1.call-update) | async-done | bytes 3145744 | tf_op jit(solution)/shard_map/all_gather | solution.py:49
  107.5 13.3 %convert_bitcast_fusion = bf16[16,64,64,64]{3,0,1,2:T(8,128)(2,1)} fusion(bf16[1,64,6,64,64]{4,3,2,0,1:T(8,128)(2,1)} %all-gather.12.cloned.1.call-done, s32[64,6]{1,0:T(8,128)S(1)} %bitcast.64, pred[64,6]{1,0:T(8,128)(4,1)S(1)} %iota_compare_fusion.1), kind=kOutput, calls=%fused_computation.20 | convolution fusion | flops 54538240 | bytes 11536256 | tf_op jit(solution)/shard_map/csb,cskn->bkcn/dot_general | solution.py:19
  120.8 18.6 %copy.21 = bf16[16,64,64,64]{3,2,1,0:T(8,128)(2,1)} copy(bf16[16,64,64,64]{3,0,1,2:T(8,128)(2,1)} %convert_bitcast_fusion) | data formatting | bytes 16777216 | tf_op jit(solution)/shard_map/convert_element_type | solution.py:20
  139.4 22.6 %reshape.78 = bf16[1024,4096]{1,0:T(8,128)(2,1)} reshape(bf16[16,64,64,64]{3,2,1,0:T(8,128)(2,1)} %copy.21) | data formatting | bytes 16777216 | tf_op jit(solution)/shard_map/reshape | solution.py:20
  162.0 127.4 %all-gather.8.cloned.1.call-done = bf16[1024,4096]{1,0:T(8,128)(2,1)} async-done(((bf16[64,4096]{1,0:T(8,128)(2,1)}), bf16[1024,4096]{1,0:T(8,128)(2,1)}) %all-gather.8.cloned.1.call-update) | async-done | bytes 8388624 | tf_op jit(solution)/shard_map/all_gather | solution.py:42
  289.4 12.0 %copy.16 = bf16[1024,4096]{0,1:T(8,128)(2,1)} copy(bf16[1024,4096]{1,0:T(8,128)(2,1)} %all-gather.8.cloned.1.call-done) | data formatting | bytes 16777216 | tf_op jit(solution)/shard_map/all_gather | solution.py:42
  301.3 82.1 %all-gather.10.cloned.1.call-done = bf16[16,24,64,64]{3,2,1,0:T(8,128)(2,1)} async-done(((bf16[1,24,64,64]{3,2,1,0:T(8,128)(2,1)}), bf16[16,24,64,64]{3,2,1,0:T(8,128)(2,1)}) %all-gather.10.cloned.1.call-update) | async-done | bytes 3145744 | tf_op jit(solution)/shard_map/all_gather | solution.py:46
  383.5 161.3 %while.11 = (s32[]{:T(128)}, f32[16,1024,64]{1,2,0:T(8,128)}, s32[16,24]{1,0:T(8,128)S(1)}, bf16[1024,64,64]{0,2,1:T(8,128)(2,1)}, bf16[16,24,64,64]{3,2,1,0:T(8,128)(2,1)}, /*index=5*/s32[16]{0:T(128)}, s32[]{:T(128)}) while((s32[]{:T(128)}, f32[16,1024,64]{1,2,0:T(8,128)}, s32[16,24]{1,0:T(8,128)S(1)}, ...), condition=%wide.region_2.3_spmd.clone, body=%wide.region_1.2_spmd.clone.sunk | while | flops 202999056 | bytes 10687693 | solution.py:33
  387.2 4.1 gather_fusion
  397.3 4.1 gather_fusion
  407.4 4.1 gather_fusion
  417.4 4.1 gather_fusion
  427.5 4.1 gather_fusion
  437.6 4.1 gather_fusion
  467.9 4.1 gather_fusion
  478.0 4.1 gather_fusion
  488.0 4.1 gather_fusion
  498.1 4.1 gather_fusion
  508.2 4.1 gather_fusion
  548.2 14.7 %convolution_convert_fusion = bf16[1024,4096]{1,0:T(8,128)(2,1)} fusion(bf16[1024,1024]{0,1:T(8,128)(2,1)S(1)} %bitcast.62, bf16[1024,4096]{1,0:T(8,128)(2,1)} %reshape.78), kind=kOutput, calls=%fused_computation.23 | convolution fusion | flops 8594128896 | bytes 18874368 | tf_op jit(solution)/shard_map/dot_general | solution.py:52
  563.0 180.6 %reduce-scatter.2.cloned.1.call-done = bf16[64,4096]{1,0:T(8,128)(2,1)} async-done(((bf16[1024,4096]{1,0:T(8,128)(2,1)}), bf16[64,4096]{1,0:T(8,128)(2,1)}) %reduce-scatter.2.cloned.1.call-update) | async-done | bytes 524304 | tf_op jit(solution)/shard_map/reduce_scatter | solution.py:57
  (139 shorter events, 128.7 us)
Async XLA Ops:
  6.5 101.0 %all-gather.12.cloned.1.call-start = ((), (), s32[]{:S(2)}) async-start(), calls=%async_computation.4 | async-start | bytes 6684672 | tf_op jit(solution)/shard_map/all_gather | solution.py:49
  7.3 282.1 %all-gather.8.cloned.1.call-start = ((), (), s32[]{:S(2)}) async-start(), calls=%async_computation.1 | async-start | bytes 8912896 | tf_op jit(solution)/shard_map/all_gather | solution.py:42
  10.6 372.8 %all-gather.10.cloned.1.call-start = ((), (), s32[]{:S(2)}) async-start(), calls=%async_computation.2 | async-start | bytes 6684672 | tf_op jit(solution)/shard_map/all_gather | solution.py:46
  11.4 732.2 %reduce-scatter.2.cloned.1.call-start = ((), (), s32[]{:S(2)}) async-start(), calls=%async_computation.3 | async-start | bytes 8912896 | tf_op jit(solution)/shard_map/reduce_scatter | solution.py:57
  563.0 180.6 %copy-start = (bf16[64,4096]{1,0:T(8,128)(2,1)S(1)}, bf16[64,4096]{1,0:T(8,128)(2,1)}, u32[]{:S(2)}) copy-start(bf16[64,4096]{1,0:T(8,128)(2,1)} %param.10) | copy-start | bytes 1572868
Sparse Core Ops, SparseCore 0:
  10.0 97.4 all-gather.11
  109.3 180.0 all-gather.7
  292.1 91.3 all-gather.9
  563.1 180.3 reduce-scatter.1
where the time goes:
time: 755 us; the launch traced here: 752 us
  waiting for transfers between devices  407 us (54%)
  local copies, waits for them, and re-layouts  162 us (21%)
  blocking collectives  76.8 us (10%)
  matrix products  63 us (8%)
  other arithmetic  28.9 us (4%)
  between operations  14.5 us (2%)
    reduce_scatter x1, waiting for transfers between devices, on_device(): lax.psum_scatter(partial_sums.astype(jnp.bfloat16), 'tp', scatter_dimensi...  181 us
    all_gather x1, waiting for transfers between devices, on_device(): gathered = lax.all_gather(normed, 'tp', axis=0, tiled=True)  127 us
    all_gather x1, waiting for transfers between devices, on_device(): lax.all_gather((up_blocks, up_rows, up_count), 'fsdp', axis=0, tiled=True)  82.1 us
    gather x16, local copies, waits for them, and re-layouts, one_column(): picked = jnp.take(row_blocks, column_r, axis=1)  66.1 us
    dynamic_slice x48, local copies, waits for them, and re-layouts, sparse_up(): stacked = lax.map(one_column, (weights, rows, count))  39.8 us
    dot_general x16, matrix products, one_column(): jnp.einsum('tsk,skn->tn', picked, masked, preferred_element_type=jnp.floa...  35 us
    all_gather x1, blocking collectives, on_device(): lax.all_gather((up_blocks, up_rows, up_count), 'fsdp', axis=0, tiled=True)  31.4 us
    all_gather x1, blocking collectives, on_device(): lax.all_gather((local_down[0], local_down[1], local_down[2]), 'fsdp', axi...  28 us
  transfers between devices with their start and end apart: 4, of which 4 were waited for; matrix products, arithmetic and copies ran while one was open for 10% of the time, Pallas kernels for 0%

commit v1 on v0

v1 whole, which is shorter than its diff:
```python
import jax
import jax.numpy as jnp
from jax import lax
from jax.sharding import PartitionSpec as P

D = 4096
FF = 16384
BLK = 64
LANES = 128


def onehot_dense(weights, rows, span):
    block_ids = jnp.arange(span, dtype=jnp.int32)
    onehot = (rows[:, :, None] == block_ids[None, None, :]).astype(jnp.bfloat16)
    dense = jnp.einsum("csb,cskn->cbkn", onehot, weights, preferred_element_type=jnp.float32)
    return dense.astype(jnp.bfloat16)


def on_device(tokens, norm_gain, up_blocks, up_rows, up_count, down_blocks, down_rows, down_count):
    x_float = tokens.astype(jnp.float32)
    scale = lax.rsqrt(jnp.mean(x_float * x_float, axis=-1, keepdims=True) + 1e-05)
    normed = (x_float * scale * norm_gain).astype(jnp.bfloat16)

    up_slots = up_blocks.shape[1]
    down_cols, down_slots = down_blocks.shape[1], down_blocks.shape[2]
    up_live = (jnp.arange(up_slots, dtype=jnp.int32)[None, :] < up_count[:, None]).astype(jnp.bfloat16)
    down_live = (
        jnp.arange(down_slots, dtype=jnp.int32)[None, None, :] < down_count[:, :, None]
    ).astype(jnp.bfloat16)
    up_w = up_blocks * up_live[:, :, None, None]
    down_w = down_blocks * down_live[:, :, :, None, None]
    n_up = up_w.size
    n_down = down_w.size
    ints = jnp.concatenate(
        [up_rows.reshape(-1), down_rows.reshape(-1)]
    ).astype(jnp.bfloat16)
    n_ints = ints.shape[0]
    pad = (-n_ints) % LANES
    packed = jnp.concatenate(
        [up_w.reshape(-1), down_w.reshape(-1), ints, jnp.zeros((pad,), jnp.bfloat16)]
    ).reshape(1, -1, LANES)
    gathered_w = lax.all_gather(packed, "fsdp", axis=0, tiled=True)
    groups = gathered_w.shape[0]
    flat = gathered_w.reshape(groups, -1)
    up_all = flat[:, :n_up].reshape(groups * up_blocks.shape[0], up_slots, BLK, BLK)
    down_all = flat[:, n_up : n_up + n_down].reshape(groups * down_cols, down_slots, BLK, BLK)
    ints_all = flat[:, n_up + n_down : n_up + n_down + n_ints].astype(jnp.int32)
    up_rows_all = ints_all[:, : up_rows.size].reshape(groups * up_blocks.shape[0], up_slots)
    down_rows_all = ints_all[:, up_rows.size :].reshape(groups * down_cols, down_slots)

    gathered = lax.all_gather(normed, "tp", axis=0, tiled=True)
    total_rows = gathered.shape[0]
    row_blocks = gathered.reshape(total_rows, D // BLK, BLK)

    dense_up = onehot_dense(up_all, up_rows_all, D // BLK)
    pre = jnp.einsum("tbk,cbkn->tcn", row_blocks, dense_up, preferred_element_type=jnp.float32)
    hidden = jax.nn.gelu(pre, approximate=True).astype(jnp.bfloat16)

    panel_span = FF // BLK // lax.axis_size("tp")
    dense_down = onehot_dense(down_all, down_rows_all, panel_span)
    partial_sums = jnp.einsum(
        "thi,jhin->tjn", hidden, dense_down, preferred_element_type=jnp.float32
    ).reshape(total_rows, D)
    summed = lax.psum_scatter(
        partial_sums.astype(jnp.bfloat16), "tp", scatter_dimension=0, tiled=True
    ).astype(jnp.float32)
    return (x_float + summed).astype(jnp.bfloat16)


def solution(mesh):
    placed = (
        P(("fsdp", "tp"), None),
        P(),
        P(("tp", "fsdp"), None, None, None),
        P(("tp", "fsdp"), None),
        P(("tp", "fsdp")),
        P("tp", "fsdp", None, None, None),
        P("tp", "fsdp", None),
        P("tp", "fsdp"),
    )
    return jax.shard_map(
        on_device, mesh=mesh, in_specs=placed, out_specs=P(("fsdp", "tp"), None), check_vma=False
    )
```

time: 755 us -> 564 us (0.75)
  local copies, waits for them, and re-layouts: 162 us -> 59 us
  blocking collectives: 76.8 us -> 0 us
  other arithmetic: 28.9 us -> 10.2 us
  matrix products: 63 us -> 75.4 us
    gather x16 -> x0, local copies, waits for them, and re-layouts: 66.1 us -> none  [one_column(): picked = jnp.take(row_blocks, column_r, axis=1)]
    all_gather x2 -> x0, blocking collectives: 59.4 us -> none  [the longest x1 31.4 us: on_device(): lax.all_gather((up_blocks, up_rows, up_count), 'fsdp', axis=0, tiled=True)]
    dynamic_slice x48 -> x0, local copies, waits for them, and re-layouts: 39.8 us -> none  [sparse_up(): stacked = lax.map(one_column, (weights, rows, count))]
    convert_element_type x17 -> x3, other arithmetic: 23.4 us -> 1.4 us  [the longest x1 0.73 us: on_device(): down_live = (jnp.arange(down_slots, dtype=jnp.int32)[None, None, :] < dow...]
    unnamed x1 -> x0, blocking collectives: 17.4 us -> none
    dot_general x18 -> x4, matrix products: 63 us -> 75.4 us  [the longest x1 31.7 us: on_device(): jnp.einsum('tbk,cbkn->tcn', row_blocks, dense_up, preferred_element_type=...]
    reshape x1 -> x5, local copies, waits for them, and re-layouts: 22.6 us -> 17.6 us  [the longest x1 8.8 us: on_device(): flat[:, :n_up].reshape(groups * up_blocks.shape[0], up_slots, BLK, BLK)]
    all_gather x2 -> x1, waiting for transfers between devices: 97.1 us -> 93.8 us  [on_device(): gathered_w = lax.all_gather(packed, 'fsdp', axis=0, tiled=True)]
  transfers between devices with their start and end apart: 4 -> 3, of which waited for: 4 -> 3; matrix products, arithmetic and copies ran while one was open for 10% -> 10% of each run, Pallas kernels for 0% -> 0%
where the time goes in v1:
time: 564 us; the launch traced here: 563 us
  waiting for transfers between devices  405 us (72%)
  matrix products  75.4 us (13%)
  local copies, waits for them, and re-layouts  59 us (10%)
  between operations  13.8 us (2%)
  other arithmetic  10.2 us (2%)
    reduce_scatter x1, waiting for transfers between devices, on_device(): lax.psum_scatter(partial_sums.astype(jnp.bfloat16), 'tp', scatter_dimensi...  184 us
    all_gather x1, waiting for transfers between devices, on_device(): gathered = lax.all_gather(normed, 'tp', axis=0, tiled=True)  127 us
    all_gather x1, waiting for transfers between devices, on_device(): gathered_w = lax.all_gather(packed, 'fsdp', axis=0, tiled=True)  93.8 us
    dot_general x1, matrix products, on_device(): jnp.einsum('tbk,cbkn->tcn', row_blocks, dense_up, preferred_element_type=...  31.7 us
    dot_general x2, matrix products, onehot_dense(): jnp.einsum('csb,cskn->cbkn', onehot, weights, preferred_element_type=jnp....  25 us
    dot_general x1, matrix products, on_device(): jnp.einsum('thi,jhin->tjn', hidden, dense_down, preferred_element_type=jn...  18.7 us
    all_gather x1, local copies, waits for them, and re-layouts, on_device(): gathered = lax.all_gather(normed, 'tp', axis=0, tiled=True)  11.9 us
    convert_element_type x1, local copies, waits for them, and re-layouts, on_device(): partial_sums.astype(jnp.bfloat16)  11.8 us
  transfers between devices with their start and end apart: 3, of which 3 were waited for; matrix products, arithmetic and copies ran while one was open for 10% of the time, Pallas kernels for 0%

profile of v1, /device:TPU:1, one launch (start us, length us, event | category | flops | bytes accessed | tf_op | source)
XLA Modules:
  0.0 563.4 jit_solution(7283157127453595981)
XLA Ops:
  7.2 1.1 broadcast_multiply_fusion.1
  8.5 0.7 fusion.29
  9.2 1.1 broadcast_multiply_fusion
  10.5 0.7 convert.9
  11.3 0.7 convert_bitcast_fusion
  12.0 5.7 %concatenate.6 = bf16[196736]{0:T(1024)(128)(2,1)} concatenate(bf16[98304]{0:T(1024)(128)(2,1)S(1)} %reshape.90, bf16[98304]{0:T(1024)(128)(2,1)S(1)} %reshape.91, bf16[24]{0:T(256)(128)(2,1)S(1)} %convert_bitcast_fusion, bf16[24]{0:T(256)(128)(2,1)S(1)} %reshape.93, bf16[80]{0:T(256)(128)(2,1)S(1)} %broadcast_in_dim.2), dimensions={0} | concatenate | bytes 786944 | tf_op jit(solution)/shard_map/concatenate | solution.py:39
  17.8 1.2 fusion.19
  19.0 2.0 fusion.21
  21.1 93.8 %all-gather.5.cloned.1.call-done = bf16[16,1537,128]{2,1,0:T(8,128)(2,1)} async-done(((bf16[1,1537,128]{2,1,0:T(8,128)(2,1)}), bf16[16,1537,128]{2,1,0:T(8,128)(2,1)}) %all-gather.5.cloned.1.call-update) | async-done | bytes 6295568 | tf_op jit(solution)/shard_map/all_gather | solution.py:42
  114.9 8.2 %copy.41 = bf16[2,8,1537,128]{3,1,2,0:T(8,128)(2,1)S(1)} copy(bf16[2,8,1537,128]{3,2,1,0:T(8,128)(2,1)} %bitcast.42) | data formatting | bytes 12591104
  123.1 2.4 fusion.30
  125.5 1.2 copy-done.1
  126.7 8.8 %reshape.96 = bf16[16,24,64,64]{3,2,1,0:T(8,128)(2,1)} reshape(bf16[16,98304]{1,0:T(8,128)(2,1)} %get-tuple-element.5) | data formatting | bytes 6291456 | tf_op jit(solution)/shard_map/reshape | solution.py:45
  135.5 8.3 %reshape.97 = bf16[64,6,64,64]{3,2,1,0:T(8,128)(2,1)} reshape(bf16[16,98304]{1,0:T(8,128)(2,1)S(1)} %get-tuple-element.6) | data formatting | bytes 6291456 | tf_op jit(solution)/shard_map/reshape | solution.py:46
  143.9 0.7 slice_convert_fusion
  144.7 12.1 %convolution_convert_fusion.1 = bf16[16,64,64,64]{3,1,2,0:T(8,128)(2,1)} fusion(bf16[16,24,64,64]{3,2,1,0:T(8,128)(2,1)} %reshape.96, s32[16,24]{1,0:T(8,128)S(1)} %get-tuple-element.7), kind=kOutput, calls=%fused_computation.6 | convolution fusion | flops 205545472 | bytes 11535872 | tf_op jit(solution)/shard_map/csb,cskn->cbkn/dot_general | solution.py:15
  156.8 12.8 %convolution_convert_fusion = bf16[64,16,64,64]{3,1,2,0:T(8,128)(2,1)} fusion(bf16[64,6,64,64]{3,2,1,0:T(8,128)(2,1)S(1)} %copy-done, s32[64,6]{1,0:T(8,128)S(1)} %eq.31), kind=kOutput, calls=%fused_computation.5 | convolution fusion | flops 54532096 | bytes 11535872 | tf_op jit(solution)/shard_map/csb,cskn->cbkn/dot_general | solution.py:15
  169.7 127.2 %all-gather.3.cloned.1.call-done = bf16[1024,4096]{1,0:T(8,128)(2,1)} async-done(((bf16[64,4096]{1,0:T(8,128)(2,1)}), bf16[1024,4096]{1,0:T(8,128)(2,1)}) %all-gather.3.cloned.1.call-update) | async-done | bytes 8388624 | tf_op jit(solution)/shard_map/all_gather | solution.py:51
  296.8 11.9 %copy.17 = bf16[1024,4096]{0,1:T(8,128)(2,1)} copy(bf16[1024,4096]{1,0:T(8,128)(2,1)} %all-gather.3.cloned.1.call-done) | data formatting | bytes 16777216 | tf_op jit(solution)/shard_map/all_gather | solution.py:51
  308.8 31.7 %fusion.15 = bf16[1024,16,64]{0,2,1:T(8,128)(2,1)S(1)} fusion(bf16[1024,64,64,1]{0,2,1,3:T(8,128)(2,1)} %bitcast.40, bf16[16,64,64,64]{3,1,2,0:T(8,128)(2,1)} %convolution_convert_fusion.1), kind=kOutput, calls=%fused_computation.18 | convolution fusion | flops 8599371776 | bytes 18874368 | tf_op jit(solution)/shard_map/tbk,cbkn->tcn/dot_general | solution.py:56
  340.4 18.7 %bitcast_convert_fusion = bf16[1024,64,64]{0,2,1:T(8,128)(2,1)} fusion(bf16[64,16,64,64]{3,1,2,0:T(8,128)(2,1)} %convolution_convert_fusion, bf16[1024,16,64]{0,2,1:T(8,128)(2,1)S(1)} %fusion.15), kind=kOutput, calls=%fused_computation | convolution fusion | flops 8594128896 | bytes 18874368 | tf_op jit(solution)/shard_map/thi,jhin->tjn/dot_general | solution.py:61
  359.2 11.8 %copy.22 = bf16[1024,4096]{1,0:T(8,128)(2,1)} copy(bf16[1024,4096]{0,1:T(8,128)(2,1)} %bitcast.41) | data formatting | bytes 16777216 | tf_op jit(solution)/shard_map/convert_element_type | solution.py:65
  371.0 183.9 %reduce-scatter.2.cloned.1.call-done = bf16[64,4096]{1,0:T(8,128)(2,1)} async-done(((bf16[1024,4096]{1,0:T(8,128)(2,1)}), bf16[64,4096]{1,0:T(8,128)(2,1)}) %reduce-scatter.2.cloned.1.call-update) | async-done | bytes 524304 | tf_op jit(solution)/shard_map/reduce_scatter | solution.py:64
  554.9 2.0 fusion.22
  (19 shorter events, 0.8 us)
Async XLA Ops:
  6.5 108.4 %all-gather.5.cloned.1.call-start = ((), (), s32[]{:S(2)}) async-start(), calls=%async_computation.2 | async-start | bytes 6719488 | tf_op jit(solution)/shard_map/all_gather | solution.py:42
  17.7 279.1 %all-gather.3.cloned.1.call-start = ((), (), s32[]{:S(2)}) async-start(), calls=%async_computation.1 | async-start | bytes 8912896 | tf_op jit(solution)/shard_map/all_gather | solution.py:51
  21.1 533.8 %reduce-scatter.2.cloned.1.call-start = ((), (), s32[]{:S(2)}) async-start(), calls=%async_computation.3 | async-start | bytes 8912896 | tf_op jit(solution)/shard_map/reduce_scatter | solution.py:64
  123.1 3.6 copy-start.1
  144.7 12.1 %copy-start = (bf16[64,6,64,64]{3,2,1,0:T(8,128)(2,1)S(1)}, bf16[64,6,64,64]{3,2,1,0:T(8,128)(2,1)}, u32[]{:S(2)}) copy-start(bf16[64,6,64,64]{3,2,1,0:T(8,128)(2,1)} %reshape.97) | copy-start | bytes 9437188
  371.0 183.9 %copy-start.2 = (bf16[64,4096]{1,0:T(8,128)(2,1)S(1)}, bf16[64,4096]{1,0:T(8,128)(2,1)}, u32[]{:S(2)}) copy-start(bf16[64,4096]{1,0:T(8,128)(2,1)} %param.8) | copy-start | bytes 1572868
Sparse Core Ops, SparseCore 0:
  17.8 97.0 all-gather.4
  116.7 180.0 all-gather.2
  371.1 183.7 reduce-scatter.1

commit v2 on v1

--- a/solution.py
+++ b/solution.py
@@ -1,7 +1,7 @@
 import jax
 import jax.numpy as jnp
 from jax import lax
-from jax.sharding import PartitionSpec as P
+from jax.sharding import Mesh, PartitionSpec as P
 
 D = 4096
 FF = 16384
@@ -39,7 +39,9 @@
     packed = jnp.concatenate(
         [up_w.reshape(-1), down_w.reshape(-1), ints, jnp.zeros((pad,), jnp.bfloat16)]
     ).reshape(1, -1, LANES)
-    gathered_w = lax.all_gather(packed, "fsdp", axis=0, tiled=True)
+    gathered_w = packed
+    for axis in ("core", "zhi", "y"):
+        gathered_w = lax.all_gather(gathered_w, axis, axis=0, tiled=True)
     groups = gathered_w.shape[0]
     flat = gathered_w.reshape(groups, -1)
     up_all = flat[:, :n_up].reshape(groups * up_blocks.shape[0], up_slots, BLK, BLK)
@@ -48,7 +50,8 @@
     up_rows_all = ints_all[:, : up_rows.size].reshape(groups * up_blocks.shape[0], up_slots)
     down_rows_all = ints_all[:, up_rows.size :].reshape(groups * down_cols, down_slots)
 
-    gathered = lax.all_gather(normed, "tp", axis=0, tiled=True)
+    gathered = lax.all_gather(normed, "zlo", axis=0, tiled=True)
+    gathered = lax.all_gather(gathered, "x", axis=0, tiled=True)
     total_rows = gathered.shape[0]
     row_blocks = gathered.reshape(total_rows, D // BLK, BLK)
 
@@ -56,28 +59,34 @@
     pre = jnp.einsum("tbk,cbkn->tcn", row_blocks, dense_up, preferred_element_type=jnp.float32)
     hidden = jax.nn.gelu(pre, approximate=True).astype(jnp.bfloat16)
 
-    panel_span = FF // BLK // lax.axis_size("tp")
+    panel_span = FF // BLK // (lax.axis_size("x") * lax.axis_size("zlo"))
     dense_down = onehot_dense(down_all, down_rows_all, panel_span)
     partial_sums = jnp.einsum(
         "thi,jhin->tjn", hidden, dense_down, preferred_element_type=jnp.float32
     ).reshape(total_rows, D)
     summed = lax.psum_scatter(
-        partial_sums.astype(jnp.bfloat16), "tp", scatter_dimension=0, tiled=True
-    ).astype(jnp.float32)
+        partial_sums.astype(jnp.bfloat16), "x", scatter_dimension=0, tiled=True
+    )
+    summed = lax.psum_scatter(summed, "zlo", scatter_dimension=0, tiled=True).astype(jnp.float32)
     return (x_float + summed).astype(jnp.bfloat16)
 
 
 def solution(mesh):
+    fsdp = ("y", "zhi", "core")
+    tp = ("x", "zlo")
+    n_fsdp, n_tp = mesh.shape["fsdp"], mesh.shape["tp"]
+    sizes = (n_fsdp // 4, 2, 2, n_tp // 4, 4)
+    fine = Mesh(mesh.devices.reshape(sizes), fsdp + tp)
     placed = (
-        P(("fsdp", "tp"), None),
+        P(fsdp + tp, None),
         P(),
-        P(("tp", "fsdp"), None, None, None),
-        P(("tp", "fsdp"), None),
-        P(("tp", "fsdp")),
-        P("tp", "fsdp", None, None, None),
-        P("tp", "fsdp", None),
-        P("tp", "fsdp"),
+        P(tp + fsdp, None, None, None),
+        P(tp + fsdp, None),
+        P(tp + fsdp),
+        P(tp, fsdp, None, None, None),
+        P(tp, fsdp, None),
+        P(tp, fsdp),
     )
     return jax.shard_map(
-        on_device, mesh=mesh, in_specs=placed, out_specs=P(("fsdp", "tp"), None), check_vma=False
+        on_device, mesh=fine, in_specs=placed, out_specs=P(fsdp + tp, None), check_vma=False
     )

time: 564 us -> 497 us (0.88)
  waiting for transfers between devices: 405 us -> 338 us
  local copies, waits for them, and re-layouts: 59 us -> 53.2 us
    reduce_scatter x1 -> x2, waiting for transfers between devices: 184 us -> 135 us  [the longest x1 84.3 us: on_device(): lax.psum_scatter(partial_sums.astype(jnp.bfloat16), 'x', scatter_dimensio...]
    all_gather x2 -> x4, waiting for transfers between devices: 221 us -> 203 us  [the longest x2 122 us: on_device(): gathered_w = lax.all_gather(gathered_w, axis, axis=0, tiled=True)]
  transfers between devices with their start and end apart: 3 -> 6, of which waited for: 3 -> 6; matrix products, arithmetic and copies ran while one was open for 10% -> 11% of each run, Pallas kernels for 0% -> 0%
where the time goes in v2:
time: 497 us; the launch traced here: 496 us
  waiting for transfers between devices  338 us (68%)
  matrix products  75.3 us (15%)
  local copies, waits for them, and re-layouts  53.2 us (11%)
  between operations  14.3 us (3%)
  other arithmetic  9.85 us (2%)
  blocking collectives  5.32 us (1%)
    all_gather x2, waiting for transfers between devices, on_device(): gathered_w = lax.all_gather(gathered_w, axis, axis=0, tiled=True)  122 us
    reduce_scatter x1, waiting for transfers between devices, on_device(): lax.psum_scatter(partial_sums.astype(jnp.bfloat16), 'x', scatter_dimensio...  84.3 us
    reduce_scatter x1, waiting for transfers between devices, on_device(): lax.psum_scatter(summed, 'zlo', scatter_dimension=0, tiled=True)  50.7 us
    all_gather x1, waiting for transfers between devices, on_device(): gathered = lax.all_gather(normed, 'zlo', axis=0, tiled=True)  47.5 us
    all_gather x1, waiting for transfers between devices, on_device(): gathered = lax.all_gather(gathered, 'x', axis=0, tiled=True)  33.3 us
    dot_general x1, matrix products, on_device(): jnp.einsum('tbk,cbkn->tcn', row_blocks, dense_up, preferred_element_type=...  31.7 us
    dot_general x2, matrix products, onehot_dense(): jnp.einsum('csb,cskn->cbkn', onehot, weights, preferred_element_type=jnp....  24.9 us
    dot_general x1, matrix products, on_device(): jnp.einsum('thi,jhin->tjn', hidden, dense_down, preferred_element_type=jn...  18.7 us
  transfers between devices with their start and end apart: 6, of which 6 were waited for; matrix products, arithmetic and copies ran while one was open for 11% of the time, Pallas kernels for 0%

profile of v2, /device:TPU:1, one launch (start us, length us, event | category | flops | bytes accessed | tf_op | source)
XLA Modules:
  0.0 495.8 jit_solution(13718692618044851233)
XLA Ops:
  7.3 1.1 broadcast_multiply_fusion.1
  8.6 0.7 fusion.29
  9.3 1.1 broadcast_multiply_fusion
  12.5 5.3 %all_gather.17 = bf16[2,1537,128]{2,1,0:T(8,128)(2,1)} all-gather(bf16[1,1537,128]{2,1,0:T(8,128)(2,1)S(1)} %bitcast.43), channel_id=1, replica_groups=mesh['y'=4,'zhi'=2,'core'=2,'x'=4,'zlo'=4] {'core'}, dimensions={0}, use_global_device_ids=true | all-gather | bytes 1180416 | tf_op jit(solution)/shard_map/all_gather | solution.py:44
  17.9 1.2 fusion.19
  19.1 1.7 fusion.21
  20.9 51.6 %all-gather.9.cloned.1.call-done = bf16[4,1537,128]{2,1,0:T(8,128)(2,1)} async-done(((bf16[2,1537,128]{2,1,0:T(8,128)(2,1)}), bf16[4,1537,128]{2,1,0:T(8,128)(2,1)}) %all-gather.9.cloned.1.call-update) | async-done | bytes 1573904 | tf_op jit(solution)/shard_map/all_gather | solution.py:44
  72.5 47.5 %all-gather.5.cloned.1.call-done = bf16[256,4096]{1,0:T(8,128)(2,1)} async-done(((bf16[64,4096]{1,0:T(8,128)(2,1)}), bf16[256,4096]{1,0:T(8,128)(2,1)}) %all-gather.5.cloned.1.call-update) | async-done | bytes 2097168 | tf_op jit(solution)/shard_map/all_gather | solution.py:53
  120.2 70.2 %all-gather.11.cloned.1.call-done = bf16[16,1537,128]{2,1,0:T(8,128)(2,1)} async-done(((bf16[4,1537,128]{2,1,0:T(8,128)(2,1)}), bf16[16,1537,128]{2,1,0:T(8,128)(2,1)}) %all-gather.11.cloned.1.call-update) | async-done | bytes 6295568 | tf_op jit(solution)/shard_map/all_gather | solution.py:44
  190.4 8.2 %copy.41 = bf16[2,8,1537,128]{3,1,2,0:T(8,128)(2,1)S(1)} copy(bf16[2,8,1537,128]{3,2,1,0:T(8,128)(2,1)} %bitcast.42) | data formatting | bytes 12591104
  198.5 2.4 fusion.30
  200.9 1.2 copy-done.1
  202.1 8.8 %reshape.96 = bf16[16,24,64,64]{3,2,1,0:T(8,128)(2,1)} reshape(bf16[16,98304]{1,0:T(8,128)(2,1)} %get-tuple-element.5) | data formatting | bytes 6291456 | tf_op jit(solution)/shard_map/reshape | solution.py:47
  210.9 8.3 %reshape.97 = bf16[64,6,64,64]{3,2,1,0:T(8,128)(2,1)} reshape(bf16[16,98304]{1,0:T(8,128)(2,1)S(1)} %get-tuple-element.6) | data formatting | bytes 6291456 | tf_op jit(solution)/shard_map/reshape | solution.py:48
  220.1 12.1 %convolution_convert_fusion.1 = bf16[16,64,64,64]{3,1,2,0:T(8,128)(2,1)} fusion(bf16[16,24,64,64]{3,2,1,0:T(8,128)(2,1)} %reshape.96, s32[16,24]{1,0:T(8,128)S(1)} %get-tuple-element.7), kind=kOutput, calls=%fused_computation.6 | convolution fusion | flops 205545472 | bytes 11535872 | tf_op jit(solution)/shard_map/csb,cskn->cbkn/dot_general | solution.py:15
  232.2 12.8 %convolution_convert_fusion = bf16[64,16,64,64]{3,1,2,0:T(8,128)(2,1)} fusion(bf16[64,6,64,64]{3,2,1,0:T(8,128)(2,1)S(1)} %copy-done, s32[64,6]{1,0:T(8,128)S(1)} %eq.31), kind=kOutput, calls=%fused_computation.5 | convolution fusion | flops 54532096 | bytes 11535872 | tf_op jit(solution)/shard_map/csb,cskn->cbkn/dot_general | solution.py:15
  245.0 33.3 %all-gather.7.cloned.1.call-done = bf16[1024,4096]{1,0:T(8,128)(2,1)} async-done(((bf16[256,4096]{1,0:T(8,128)(2,1)}), bf16[1024,4096]{1,0:T(8,128)(2,1)}) %all-gather.7.cloned.1.call-update) | async-done | bytes 8388624 | tf_op jit(solution)/shard_map/all_gather | solution.py:54
  278.3 12.0 %copy.17 = bf16[1024,4096]{0,1:T(8,128)(2,1)} copy(bf16[1024,4096]{1,0:T(8,128)(2,1)} %all-gather.7.cloned.1.call-done) | data formatting | bytes 16777216 | tf_op jit(solution)/shard_map/all_gather | solution.py:54
  290.3 31.7 %fusion.15 = bf16[1024,16,64]{0,2,1:T(8,128)(2,1)S(1)} fusion(bf16[1024,64,64,1]{0,2,1,3:T(8,128)(2,1)} %bitcast.40, bf16[16,64,64,64]{3,1,2,0:T(8,128)(2,1)} %convolution_convert_fusion.1), kind=kOutput, calls=%fused_computation.18 | convolution fusion | flops 8599371776 | bytes 18874368 | tf_op jit(solution)/shard_map/tbk,cbkn->tcn/dot_general | solution.py:59
  321.9 18.7 %bitcast_convert_fusion = bf16[1024,64,64]{0,2,1:T(8,128)(2,1)} fusion(bf16[64,16,64,64]{3,1,2,0:T(8,128)(2,1)} %convolution_convert_fusion, bf16[1024,16,64]{0,2,1:T(8,128)(2,1)S(1)} %fusion.15), kind=kOutput, calls=%fused_computation | convolution fusion | flops 8594128896 | bytes 18874368 | tf_op jit(solution)/shard_map/thi,jhin->tjn/dot_general | solution.py:64
  340.6 11.3 %copy.22 = bf16[1024,4096]{1,0:T(8,128)(2,1)} copy(bf16[1024,4096]{0,1:T(8,128)(2,1)} %bitcast.41) | data formatting | bytes 16777216 | tf_op jit(solution)/shard_map/convert_element_type | solution.py:68
  352.0 84.3 %reduce-scatter.3.cloned.1.call-done = bf16[256,4096]{1,0:T(8,128)(2,1)} async-done(((bf16[1024,4096]{1,0:T(8,128)(2,1)}), bf16[256,4096]{1,0:T(8,128)(2,1)}) %reduce-scatter.3.cloned.1.call-update) | async-done | bytes 2097168 | tf_op jit(solution)/shard_map/reduce_scatter | solution.py:67
  436.3 50.7 %reduce-scatter.5.cloned.1.call-done = bf16[64,4096]{1,0:T(8,128)(2,1)} async-done(((bf16[256,4096]{1,0:T(8,128)(2,1)}), bf16[64,4096]{1,0:T(8,128)(2,1)}) %reduce-scatter.5.cloned.1.call-update) | async-done | bytes 524304 | tf_op jit(solution)/shard_map/reduce_scatter | solution.py:70
  487.0 2.0 fusion.22
  (31 shorter events, 3.4 us)
Async XLA Ops:
  6.5 12.6 %copy-start.2 = (bf16[64,4096]{1,0:T(8,128)(2,1)S(1)}, bf16[64,4096]{1,0:T(8,128)(2,1)}, u32[]{:S(2)}) copy-start(bf16[64,4096]{1,0:T(8,128)(2,1)} %param.8) | copy-start | bytes 1572868
  6.5 65.9 %all-gather.9.cloned.1.call-start = ((), (), s32[]{:S(2)}) async-start(), calls=%async_computation.4 | async-start | bytes 2371584 | tf_op jit(solution)/shard_map/all_gather | solution.py:44
  17.8 102.3 %all-gather.5.cloned.1.call-start = ((), (), s32[]{:S(2)}) async-start(), calls=%async_computation.2 | async-start | bytes 2621440 | tf_op jit(solution)/shard_map/all_gather | solution.py:53
  20.9 169.5 %all-gather.11.cloned.1.call-start = ((), (), s32[]{:S(2)}) async-start(), calls=%async_computation.5 | async-start | bytes 7905280 | tf_op jit(solution)/shard_map/all_gather | solution.py:44
  72.5 205.8 %all-gather.7.cloned.1.call-start = ((), (), s32[]{:S(2)}) async-start(), calls=%async_computation.3 | async-start | bytes 10485760 | tf_op jit(solution)/shard_map/all_gather | solution.py:54
  120.1 316.1 %reduce-scatter.3.cloned.1.call-start = ((), (), s32[]{:S(2)}) async-start(), calls=%async_computation.6 | async-start | bytes 10485760 | tf_op jit(solution)/shard_map/reduce_scatter | solution.py:67
  198.5 3.6 copy-start.1
  220.1 12.1 %copy-start = (bf16[64,6,64,64]{3,2,1,0:T(8,128)(2,1)S(1)}, bf16[64,6,64,64]{3,2,1,0:T(8,128)(2,1)}, u32[]{:S(2)}) copy-start(bf16[64,6,64,64]{3,2,1,0:T(8,128)(2,1)} %reshape.97) | copy-start | bytes 9437188
  351.9 135.1 %copy-start.3 = (bf16[64,4096]{1,0:T(8,128)(2,1)S(1)}, bf16[64,4096]{1,0:T(8,128)(2,1)}, u32[]{:S(2)}) copy-start(bf16[64,4096]{1,0:T(8,128)(2,1)} %param.8) | copy-start | bytes 1572868
  351.9 135.1 %reduce-scatter.5.cloned.1.call-start = ((), (), s32[]{:S(2)}) async-start(), calls=%async_computation.7 | async-start | bytes 2621440 | tf_op jit(solution)/shard_map/reduce_scatter | solution.py:70
Sparse Core Ops, SparseCore 0:
  17.9 54.4 all-gather.8
  74.3 45.7 all-gather.4
  121.9 68.4 all-gather.10
  192.0 86.2 all-gather.6
  352.0 84.1 reduce-scatter.2
  438.6 48.3 reduce-scatter.4

commit v3 on v2

--- a/solution.py
+++ b/solution.py
@@ -14,6 +14,17 @@
     onehot = (rows[:, :, None] == block_ids[None, None, :]).astype(jnp.bfloat16)
     dense = jnp.einsum("csb,cskn->cbkn", onehot, weights, preferred_element_type=jnp.float32)
     return dense.astype(jnp.bfloat16)
+
+
+def permute_gather(piece, axis):
+    size = lax.axis_size(axis)
+    me = lax.axis_index(axis)
+    whole = jnp.zeros((size,) + piece.shape, piece.dtype)
+    whole = lax.dynamic_update_index_in_dim(whole, piece, me, 0)
+    for shift in range(1, size):
+        moved = lax.ppermute(piece, axis, [(i, (i + shift) % size) for i in range(size)])
+        whole = lax.dynamic_update_index_in_dim(whole, moved, (me - shift) % size, 0)
+    return whole.reshape((size * piece.shape[0],) + piece.shape[1:])
 
 
 def on_device(tokens, norm_gain, up_blocks, up_rows, up_count, down_blocks, down_rows, down_count):
@@ -39,9 +50,9 @@
     packed = jnp.concatenate(
         [up_w.reshape(-1), down_w.reshape(-1), ints, jnp.zeros((pad,), jnp.bfloat16)]
     ).reshape(1, -1, LANES)
-    gathered_w = packed
-    for axis in ("core", "zhi", "y"):
-        gathered_w = lax.all_gather(gathered_w, axis, axis=0, tiled=True)
+    gathered_w = lax.all_gather(packed, "core", axis=0, tiled=True)
+    gathered_w = permute_gather(gathered_w, "zhi")
+    gathered_w = permute_gather(gathered_w, "y")
     groups = gathered_w.shape[0]
     flat = gathered_w.reshape(groups, -1)
     up_all = flat[:, :n_up].reshape(groups * up_blocks.shape[0], up_slots, BLK, BLK)

time: 497 us -> 461 us (0.928); the launches traced: 496 us -> 453 us
  waiting for transfers between devices: 338 us -> 263 us
  local copies, waits for them, and re-layouts: 53.2 us -> 76 us
  starting transfers between devices: 0.2 us -> 10.7 us
    all_gather x2 -> x0, waiting for transfers between devices: 122 us -> none  [on_device(): gathered_w = lax.all_gather(gathered_w, axis, axis=0, tiled=True)]
    ppermute x0 -> x4, waiting for transfers between devices: none -> 74.5 us  [permute_gather(): lax.ppermute(piece, axis, [(i, (i + shift) % size) for i in range(size)])]
    all_gather x1, waiting for transfers between devices: 47.5 us -> 0.01 us  [on_device(): gathered = lax.all_gather(normed, 'zlo', axis=0, tiled=True)]
    all_gather x1, waiting for transfers between devices: 33.3 us -> 53.1 us  [on_device(): gathered = lax.all_gather(gathered, 'x', axis=0, tiled=True)]
    dynamic_update_slice x0 -> x7, local copies, waits for them, and re-layouts: none -> 14.5 us  [the longest x5 7.82 us: permute_gather(): lax.dynamic_update_index_in_dim(whole, moved, (me - shift) % size, 0)]
    ppermute x0 -> x4, starting transfers between devices: none -> 10.6 us  [permute_gather(): lax.ppermute(piece, axis, [(i, (i + shift) % size) for i in range(size)])]
    all_gather x0 -> x1, local copies, waits for them, and re-layouts: none -> 6.42 us  [on_device(): gathered_w = lax.all_gather(packed, 'core', axis=0, tiled=True)]
  transfers between devices with their start and end apart: 6 -> 8, of which waited for: 6 -> 7; matrix products, arithmetic and copies ran while one was open for 11% -> 16% of each run, Pallas kernels for 0% -> 0%
where the time goes in v3:
time: 461 us; the launch traced here: 453 us
  waiting for transfers between devices  263 us (57%)
  local copies, waits for them, and re-layouts  76 us (16%)
  matrix products  76 us (16%)
  between operations  14.4 us (3%)
  starting transfers between devices  10.7 us (2%)
  other arithmetic  8.08 us (2%)
  blocking collectives  5.19 us (1%)
    reduce_scatter x1, waiting for transfers between devices, on_device(): lax.psum_scatter(partial_sums.astype(jnp.bfloat16), 'x', scatter_dimensio...  84.3 us
    ppermute x4, waiting for transfers between devices, permute_gather(): lax.ppermute(piece, axis, [(i, (i + shift) % size) for i in range(size)])  74.5 us
    all_gather x1, waiting for transfers between devices, on_device(): gathered = lax.all_gather(gathered, 'x', axis=0, tiled=True)  53.1 us
    reduce_scatter x1, waiting for transfers between devices, on_device(): lax.psum_scatter(summed, 'zlo', scatter_dimension=0, tiled=True)  50.7 us
    dot_general x1, matrix products, on_device(): jnp.einsum('tbk,cbkn->tcn', row_blocks, dense_up, preferred_element_type=...  31.9 us
    dot_general x2, matrix products, onehot_dense(): jnp.einsum('csb,cskn->cbkn', onehot, weights, preferred_element_type=jnp....  25.3 us
    dot_general x1, matrix products, on_device(): jnp.einsum('thi,jhin->tjn', hidden, dense_down, preferred_element_type=jn...  18.7 us
    all_gather x1, local copies, waits for them, and re-layouts, on_device(): gathered = lax.all_gather(gathered, 'x', axis=0, tiled=True)  11.9 us
  transfers between devices with their start and end apart: 8, of which 7 were waited for; matrix products, arithmetic and copies ran while one was open for 16% of the time, Pallas kernels for 0%

profile of v3, /device:TPU:1, one launch (start us, length us, event | category | flops | bytes accessed | tf_op | source)
XLA Modules:
  0.0 453.1 jit_solution(9548094344440936409)
XLA Ops:
  12.5 5.2 %all_gather.11 = bf16[2,1537,128]{2,1,0:T(8,128)(2,1)S(1)} all-gather(bf16[1,1537,128]{2,1,0:T(8,128)(2,1)S(1)} %bitcast.61), channel_id=1, replica_groups=mesh['y'=4,'zhi'=2,'core'=2,'x'=4,'zlo'=4] {'core'}, dimensions={0}, use_global_device_ids=true | all-gather | bytes 1180416 | tf_op jit(solution)/shard_map/all_gather | solution.py:53
  17.7 6.4 %copy.26 = bf16[2,1537,128]{2,0,1:T(2,128)(2,1)} copy(bf16[2,1537,128]{2,1,0:T(8,128)(2,1)S(1)} %all_gather.11) | data formatting | bytes 1573888 | tf_op jit(solution)/shard_map/all_gather | solution.py:53
  24.1 5.2 %collective-permute-start = (bf16[2,1537,128]{2,0,1:T(2,128)(2,1)}, bf16[2,1537,128]{2,0,1:T(2,128)(2,1)}, u32[]{:S(2)}, u32[]{:S(2)}) collective-permute-start(bf16[2,1537,128]{2,0,1:T(2,128)(2,1)} %copy.26), channel_id=1, source_target_pairs={{0,32},{32,0},{1,33},{33,1},{2,34},{34,2},{3,35},{35,3},{4,36},{36... | collective-permute-start | bytes 2360840 | tf_op jit(solution)/shard_map/ppermute | solution.py:25
  30.4 6.4 %copy_dynamic-update-slice_fusion.3 = bf16[2,2,1537,128]{3,1,0,2:T(2,128)(2,1)S(1)} fusion(bf16[2,2,1537,128]{3,1,0,2:T(2,128)(2,1)S(1)} %broadcast_in_dim.41, s32[]{:T(128)S(6)} %select_n.39, bf16[1,2,1537,128]{3,2,1,0:T(8,128)(2,1)S(1)} %bitcast.56), kind=kLoop, calls=%fused_computation.32 | loop fusion | bytes 1577476 | tf_op jit(solution)/shard_map/jit(dynamic_update_index_in_dim)/dynamic_update_slice | solution.py:23
  36.8 13.6 %collective-permute-done = bf16[2,1537,128]{2,0,1:T(2,128)(2,1)} collective-permute-done((bf16[2,1537,128]{2,0,1:T(2,128)(2,1)}, bf16[2,1537,128]{2,0,1:T(2,128)(2,1)}, u32[]{:S(2)}, u32[]{:S(2)}) %collective-permute-start) | collective-permute-done | bytes 786976 | tf_op jit(solution)/shard_map/ppermute | solution.py:25
  50.4 2.3 bitcast_dynamic-update-slice_fusion.1
  55.2 2.7 collective-permute-start.2
  60.4 16.9 %collective-permute-done.1 = bf16[4,1537,128]{2,0,1:T(4,128)(2,1)} collective-permute-done((bf16[4,1537,128]{2,0,1:T(4,128)(2,1)S(1)}, bf16[4,1537,128]{2,0,1:T(4,128)(2,1)}, u32[]{:S(2)}, u32[]{:S(2)}) %collective-permute-start.1) | collective-permute-done | bytes 1573920 | tf_op jit(solution)/shard_map/ppermute | solution.py:25
  79.1 32.8 %collective-permute-done.2 = bf16[4,1537,128]{2,0,1:T(4,128)(2,1)} collective-permute-done((bf16[4,1537,128]{2,0,1:T(4,128)(2,1)S(1)}, bf16[4,1537,128]{2,0,1:T(4,128)(2,1)}, u32[]{:S(2)}, u32[]{:S(2)}) %collective-permute-start.2) | collective-permute-done | bytes 1573920 | tf_op jit(solution)/shard_map/ppermute | solution.py:25
  113.8 11.2 %collective-permute-done.3 = bf16[4,1537,128]{2,0,1:T(4,128)(2,1)} collective-permute-done((bf16[4,1537,128]{2,0,1:T(4,128)(2,1)S(1)}, bf16[4,1537,128]{2,0,1:T(4,128)(2,1)}, u32[]{:S(2)}, u32[]{:S(2)}) %collective-permute-start.3) | collective-permute-done | bytes 1573920 | tf_op jit(solution)/shard_map/ppermute | solution.py:25
  126.7 7.1 %copy.59 = bf16[2,8,1537,128]{3,1,2,0:T(8,128)(2,1)} copy(bf16[2,8,1537,128]{3,2,1,0:T(8,128)(2,1)S(1)} %bitcast.51) | data formatting | bytes 12591104
  133.9 4.9 %fusion.30 = (bf16[16,98304]{1,0:T(8,128)(2,1)}, bf16[16,98304]{1,0:T(8,128)(2,1)S(1)}) fusion(bf16[16,196736]{1,0:T(8,128)(2,1)} %bitcast.52), kind=kLoop, calls=%fused_computation.47 | loop fusion | bytes 12582912 | tf_op jit(solution)/shard_map/slice | solution.py:58
  138.8 8.8 %reshape.97 = bf16[16,24,64,64]{3,2,1,0:T(8,128)(2,1)} reshape(bf16[16,98304]{1,0:T(8,128)(2,1)} %get-tuple-element.5) | data formatting | bytes 6291456 | tf_op jit(solution)/shard_map/reshape | solution.py:58
  147.6 8.3 %reshape.98 = bf16[64,6,64,64]{3,2,1,0:T(8,128)(2,1)} reshape(bf16[16,98304]{1,0:T(8,128)(2,1)S(1)} %get-tuple-element.6) | data formatting | bytes 6291456 | tf_op jit(solution)/shard_map/reshape | solution.py:59
  156.7 12.5 %convolution_convert_fusion.1 = bf16[16,64,64,64]{3,1,2,0:T(8,128)(2,1)} fusion(bf16[16,24,64,64]{3,2,1,0:T(8,128)(2,1)} %reshape.97, s32[16,24]{1,0:T(8,128)S(1)} %get-tuple-element.7), kind=kOutput, calls=%fused_computation.6 | convolution fusion | flops 205545472 | bytes 11535872 | tf_op jit(solution)/shard_map/csb,cskn->cbkn/dot_general | solution.py:15
  169.2 12.8 %convolution_convert_fusion = bf16[64,16,64,64]{3,1,2,0:T(8,128)(2,1)} fusion(bf16[64,6,64,64]{3,2,1,0:T(8,128)(2,1)S(1)} %copy-done, s32[64,6]{1,0:T(8,128)S(1)} %eq.36), kind=kOutput, calls=%fused_computation.5 | convolution fusion | flops 54532096 | bytes 11535872 | tf_op jit(solution)/shard_map/csb,cskn->cbkn/dot_general | solution.py:15
  182.1 53.1 %all-gather.5.cloned.1.call-done = bf16[1024,4096]{1,0:T(8,128)(2,1)} async-done(((bf16[256,4096]{1,0:T(8,128)(2,1)}), bf16[1024,4096]{1,0:T(8,128)(2,1)}) %all-gather.5.cloned.1.call-update) | async-done | bytes 8388624 | tf_op jit(solution)/shard_map/all_gather | solution.py:65
  235.2 11.9 %copy.24 = bf16[1024,4096]{0,1:T(8,128)(2,1)} copy(bf16[1024,4096]{1,0:T(8,128)(2,1)} %all-gather.5.cloned.1.call-done) | data formatting | bytes 16777216 | tf_op jit(solution)/shard_map/all_gather | solution.py:65
  247.1 31.9 %fusion.15 = bf16[1024,16,64]{0,2,1:T(8,128)(2,1)S(1)} fusion(bf16[1024,64,64,1]{0,2,1,3:T(8,128)(2,1)} %bitcast.54, bf16[16,64,64,64]{3,1,2,0:T(8,128)(2,1)} %convolution_convert_fusion.1), kind=kOutput, calls=%fused_computation.18 | convolution fusion | flops 8599371776 | bytes 18874368 | tf_op jit(solution)/shard_map/tbk,cbkn->tcn/dot_general | solution.py:70
  279.0 18.7 %bitcast_convert_fusion = bf16[1024,64,64]{0,2,1:T(8,128)(2,1)} fusion(bf16[64,16,64,64]{3,1,2,0:T(8,128)(2,1)} %convolution_convert_fusion, bf16[1024,16,64]{0,2,1:T(8,128)(2,1)S(1)} %fusion.15), kind=kOutput, calls=%fused_computation | convolution fusion | flops 8594128896 | bytes 18874368 | tf_op jit(solution)/shard_map/thi,jhin->tjn/dot_general | solution.py:75
  297.7 11.3 %copy.36 = bf16[1024,4096]{1,0:T(8,128)(2,1)} copy(bf16[1024,4096]{0,1:T(8,128)(2,1)} %bitcast.55) | data formatting | bytes 16777216 | tf_op jit(solution)/shard_map/convert_element_type | solution.py:79
  309.1 84.3 %reduce-scatter.3.cloned.1.call-done = bf16[256,4096]{1,0:T(8,128)(2,1)} async-done(((bf16[1024,4096]{1,0:T(8,128)(2,1)}), bf16[256,4096]{1,0:T(8,128)(2,1)}) %reduce-scatter.3.cloned.1.call-update) | async-done | bytes 2097168 | tf_op jit(solution)/shard_map/reduce_scatter | solution.py:78
  393.4 50.7 %reduce-scatter.5.cloned.1.call-done = bf16[64,4096]{1,0:T(8,128)(2,1)} async-done(((bf16[256,4096]{1,0:T(8,128)(2,1)}), bf16[64,4096]{1,0:T(8,128)(2,1)}) %reduce-scatter.5.cloned.1.call-update) | async-done | bytes 524304 | tf_op jit(solution)/shard_map/reduce_scatter | solution.py:81
  444.2 2.0 fusion.22
  (43 shorter events, 17.5 us)
Async XLA Ops:
  6.5 22.8 %copy-start.1 = (bf16[64,4096]{1,0:T(8,128)(2,1)S(1)}, bf16[64,4096]{1,0:T(8,128)(2,1)}, u32[]{:S(2)}) copy-start(bf16[64,4096]{1,0:T(8,128)(2,1)} %param.8) | copy-start | bytes 1572868
  6.5 47.6 %copy-start.3 = (f32[4096]{0:T(1024)S(1)}, f32[4096]{0:T(1024)}, u32[]{:S(2)}) copy-start(f32[4096]{0:T(1024)} %param.9) | copy-start | bytes 49156
  6.5 127.3 %all-gather.3.cloned.1.call-start = ((), (), s32[]{:S(2)}) async-start(), calls=%async_computation.2 | async-start | bytes 2621440 | tf_op jit(solution)/shard_map/all_gather | solution.py:64
  24.1 26.3 %collective-permute-start = (bf16[2,1537,128]{2,0,1:T(2,128)(2,1)}, bf16[2,1537,128]{2,0,1:T(2,128)(2,1)}, u32[]{:S(2)}, u32[]{:S(2)}) collective-permute-start(bf16[2,1537,128]{2,0,1:T(2,128)(2,1)} %copy.26), channel_id=1, source_target_pairs={{0,32},{32,0},{1,33},{33,1},{2,34},{34,2},{3,35},{35,3},{4,36},{36... | collective-permute-start | bytes 2360840 | tf_op jit(solution)/shard_map/ppermute | solution.py:25
  52.7 24.7 %collective-permute-start.1 = (bf16[4,1537,128]{2,0,1:T(4,128)(2,1)S(1)}, bf16[4,1537,128]{2,0,1:T(4,128)(2,1)}, u32[]{:S(2)}, u32[]{:S(2)}) collective-permute-start(bf16[4,1537,128]{2,0,1:T(4,128)(2,1)S(1)} %bitcast.58), channel_id=1, source_target_pairs={{0,64},{64,128},{128,192},{192,0},{1,65},{65,129},{129,193},{193,1... | collective-permute-start | bytes 4721672 | tf_op jit(solution)/shard_map/ppermute | solution.py:25
  55.2 180.0 %all-gather.5.cloned.1.call-start = ((), (), s32[]{:S(2)}) async-start(), calls=%async_computation.3 | async-start | bytes 10485760 | tf_op jit(solution)/shard_map/all_gather | solution.py:65
  55.2 56.8 %collective-permute-start.2 = (bf16[4,1537,128]{2,0,1:T(4,128)(2,1)S(1)}, bf16[4,1537,128]{2,0,1:T(4,128)(2,1)}, u32[]{:S(2)}, u32[]{:S(2)}) collective-permute-start(bf16[4,1537,128]{2,0,1:T(4,128)(2,1)S(1)} %bitcast.59), channel_id=1, source_target_pairs={{0,128},{64,192},{128,0},{192,64},{1,129},{65,193},{129,1},{193,65... | collective-permute-start | bytes 4721672 | tf_op jit(solution)/shard_map/ppermute | solution.py:25
  57.9 67.0 %collective-permute-start.3 = (bf16[4,1537,128]{2,0,1:T(4,128)(2,1)S(1)}, bf16[4,1537,128]{2,0,1:T(4,128)(2,1)}, u32[]{:S(2)}, u32[]{:S(2)}) collective-permute-start(bf16[4,1537,128]{2,0,1:T(4,128)(2,1)S(1)} %bitcast.60), channel_id=1, source_target_pairs={{0,192},{64,0},{128,64},{192,128},{1,193},{65,1},{129,65},{193,129... | collective-permute-start | bytes 4721672 | tf_op jit(solution)/shard_map/ppermute | solution.py:25
  133.9 259.6 %reduce-scatter.3.cloned.1.call-start = ((), (), s32[]{:S(2)}) async-start(), calls=%async_computation.4 | async-start | bytes 10485760 | tf_op jit(solution)/shard_map/reduce_scatter | solution.py:78
  156.7 12.5 %copy-start = (bf16[64,6,64,64]{3,2,1,0:T(8,128)(2,1)S(1)}, bf16[64,6,64,64]{3,2,1,0:T(8,128)(2,1)}, u32[]{:S(2)}) copy-start(bf16[64,6,64,64]{3,2,1,0:T(8,128)(2,1)} %reshape.98) | copy-start | bytes 9437188
  309.1 135.1 %copy-start.2 = (bf16[64,4096]{1,0:T(8,128)(2,1)S(1)}, bf16[64,4096]{1,0:T(8,128)(2,1)}, u32[]{:S(2)}) copy-start(bf16[64,4096]{1,0:T(8,128)(2,1)} %param.8) | copy-start | bytes 1572868
  309.1 135.1 %reduce-scatter.5.cloned.1.call-start = ((), (), s32[]{:S(2)}) async-start(), calls=%async_computation.5 | async-start | bytes 2621440 | tf_op jit(solution)/shard_map/reduce_scatter | solution.py:81
Sparse Core Ops, SparseCore 0:
  55.3 64.2 all-gather.2
  134.0 101.1 all-gather.4
  309.2 84.1 reduce-scatter.2
  395.8 48.3 reduce-scatter.4

commit v4 on v3

--- a/solution.py
+++ b/solution.py
@@ -50,6 +50,7 @@
     packed = jnp.concatenate(
         [up_w.reshape(-1), down_w.reshape(-1), ints, jnp.zeros((pad,), jnp.bfloat16)]
     ).reshape(1, -1, LANES)
+    normed, packed = lax.optimization_barrier((normed, packed))
     gathered_w = lax.all_gather(packed, "core", axis=0, tiled=True)
     gathered_w = permute_gather(gathered_w, "zhi")
     gathered_w = permute_gather(gathered_w, "y")
@@ -61,24 +62,29 @@
     up_rows_all = ints_all[:, : up_rows.size].reshape(groups * up_blocks.shape[0], up_slots)
     down_rows_all = ints_all[:, up_rows.size :].reshape(groups * down_cols, down_slots)
 
-    gathered = lax.all_gather(normed, "zlo", axis=0, tiled=True)
-    gathered = lax.all_gather(gathered, "x", axis=0, tiled=True)
-    total_rows = gathered.shape[0]
-    row_blocks = gathered.reshape(total_rows, D // BLK, BLK)
-
     dense_up = onehot_dense(up_all, up_rows_all, D // BLK)
-    pre = jnp.einsum("tbk,cbkn->tcn", row_blocks, dense_up, preferred_element_type=jnp.float32)
-    hidden = jax.nn.gelu(pre, approximate=True).astype(jnp.bfloat16)
-
     panel_span = FF // BLK // (lax.axis_size("x") * lax.axis_size("zlo"))
     dense_down = onehot_dense(down_all, down_rows_all, panel_span)
-    partial_sums = jnp.einsum(
-        "thi,jhin->tjn", hidden, dense_down, preferred_element_type=jnp.float32
-    ).reshape(total_rows, D)
-    summed = lax.psum_scatter(
-        partial_sums.astype(jnp.bfloat16), "x", scatter_dimension=0, tiled=True
-    )
-    summed = lax.psum_scatter(summed, "zlo", scatter_dimension=0, tiled=True).astype(jnp.float32)
+
+    halves = 2
+    part = normed.shape[0] // halves
+    outs = []
+    for h in range(halves):
+        rows = normed[h * part : (h + 1) * part]
+        gathered = lax.all_gather(rows, "zlo", axis=0, tiled=True)
+        gathered = lax.all_gather(gathered, "x", axis=0, tiled=True)
+        total_rows = gathered.shape[0]
+        row_blocks = gathered.reshape(total_rows, D // BLK, BLK)
+        pre = jnp.einsum("tbk,cbkn->tcn", row_blocks, dense_up, preferred_element_type=jnp.float32)
+        hidden = jax.nn.gelu(pre, approximate=True).astype(jnp.bfloat16)
+        partial_sums = jnp.einsum(
+            "thi,jhin->tjn", hidden, dense_down, preferred_element_type=jnp.float32
+        ).reshape(total_rows, D)
+        summed = lax.psum_scatter(
+            partial_sums.astype(jnp.bfloat16), "x", scatter_dimension=0, tiled=True
+        )
+        outs.append(lax.psum_scatter(summed, "zlo", scatter_dimension=0, tiled=True))
+    summed = jnp.concatenate(outs, axis=0).astype(jnp.float32)
     return (x_float + summed).astype(jnp.bfloat16)
 
 

time: 461 us -> 519 us (1.13)
  local copies, waits for them, and re-layouts: 76 us -> 131 us
  waiting for transfers between devices: 263 us -> 274 us
  matrix products: 76 us -> 69 us
    all_gather x1 -> x2, waiting for transfers between devices: 53.1 us -> 0.02 us  [on_device(): gathered = lax.all_gather(gathered, 'x', axis=0, tiled=True)]
    convert_element_type x0 -> x2, local copies, waits for them, and re-layouts: none -> 46.8 us  [onehot_dense(): return dense.astype(jnp.bfloat16)]
    all_gather x1 -> x2, waiting for transfers between devices: 0.01 us -> 35.9 us  [on_device(): gathered = lax.all_gather(rows, 'zlo', axis=0, tiled=True)]
    reduce_scatter x1 -> x2, waiting for transfers between devices: 50.7 us -> 68.6 us  [on_device(): lax.psum_scatter(summed, 'zlo', scatter_dimension=0, tiled=True)]
    ppermute x4, waiting for transfers between devices: 74.5 us -> 92.3 us  [permute_gather(): lax.ppermute(piece, axis, [(i, (i + shift) % size) for i in range(size)])]
    dot_general x1 -> x2, matrix products: 31.9 us -> 20.3 us  [on_device(): jnp.einsum('tbk,cbkn->tcn', row_blocks, dense_up, preferred_element_type=...]
    reduce_scatter x1 -> x2, waiting for transfers between devices: 84.3 us -> 76.2 us  [on_device(): lax.psum_scatter(partial_sums.astype(jnp.bfloat16), 'x', scatter_dimensio...]
    dot_general x1 -> x2, matrix products: 18.7 us -> 20.8 us  [on_device(): jnp.einsum('thi,jhin->tjn', hidden, dense_down, preferred_element_type=jn...]
  transfers between devices with their start and end apart: 8 -> 12, of which waited for: 7 -> 9; matrix products, arithmetic and copies ran while one was open for 16% -> 39% of each run, Pallas kernels for 0% -> 0%
where the time goes in v4:
time: 519 us; the launch traced here: 509 us
  waiting for transfers between devices  274 us (53%)
  local copies, waits for them, and re-layouts  131 us (25%)
  matrix products  69 us (13%)
  between operations  14.5 us (3%)
  other arithmetic  8.7 us (2%)
  starting transfers between devices  8.56 us (2%)
    ppermute x4, waiting for transfers between devices, permute_gather(): lax.ppermute(piece, axis, [(i, (i + shift) % size) for i in range(size)])  92.3 us
    reduce_scatter x2, waiting for transfers between devices, on_device(): lax.psum_scatter(partial_sums.astype(jnp.bfloat16), 'x', scatter_dimensio...  76.2 us
    reduce_scatter x2, waiting for transfers between devices, on_device(): lax.psum_scatter(summed, 'zlo', scatter_dimension=0, tiled=True)  68.6 us
    convert_element_type x2, local copies, waits for them, and re-layouts, onehot_dense(): return dense.astype(jnp.bfloat16)  46.8 us
    all_gather x2, waiting for transfers between devices, on_device(): gathered = lax.all_gather(rows, 'zlo', axis=0, tiled=True)  35.9 us
    dot_general x2, matrix products, onehot_dense(): jnp.einsum('csb,cskn->cbkn', onehot, weights, preferred_element_type=jnp....  27.9 us
    dot_general x2, matrix products, on_device(): jnp.einsum('thi,jhin->tjn', hidden, dense_down, preferred_element_type=jn...  20.8 us
    dot_general x2, matrix products, on_device(): jnp.einsum('tbk,cbkn->tcn', row_blocks, dense_up, preferred_element_type=...  20.3 us
  transfers between devices with their start and end apart: 12, of which 9 were waited for; matrix products, arithmetic and copies ran while one was open for 39% of the time, Pallas kernels for 0%

profile of v4, /device:TPU:1, one launch (start us, length us, event | category | flops | bytes accessed | tf_op | source)
XLA Modules:
  0.0 508.9 jit_solution(12687885201322824714)
XLA Ops:
  16.6 35.9 %all-gather.5.cloned.1.call-done = bf16[128,4096]{1,0:T(8,128)(2,1)} async-done(((bf16[32,4096]{1,0:T(8,128)(2,1)}), bf16[128,4096]{1,0:T(8,128)(2,1)}) %all-gather.5.cloned.1.call-update) | async-done | bytes 1048592 | tf_op jit(solution)/shard_map/all_gather | solution.py:74
  56.1 6.4 %copy.29 = bf16[2,1537,128]{2,0,1:T(2,128)(2,1)} copy(bf16[2,1537,128]{2,1,0:T(8,128)(2,1)S(1)} %all_gather.17) | data formatting | bytes 1573888 | tf_op jit(solution)/shard_map/all_gather | solution.py:54
  66.4 6.4 %copy_dynamic-update-slice_fusion.3 = bf16[2,2,1537,128]{3,1,0,2:T(2,128)(2,1)S(1)} fusion(bf16[2,2,1537,128]{3,1,0,2:T(2,128)(2,1)S(1)} %broadcast_in_dim.42, s32[]{:T(128)S(6)} %select_n.39, bf16[1,2,1537,128]{3,2,1,0:T(8,128)(2,1)S(1)} %bitcast.75), kind=kLoop, calls=%fused_computation.39 | loop fusion | bytes 1577476 | tf_op jit(solution)/shard_map/jit(dynamic_update_index_in_dim)/dynamic_update_slice | solution.py:23
  72.9 37.2 %collective-permute-done = bf16[2,1537,128]{2,0,1:T(2,128)(2,1)S(1)} collective-permute-done((bf16[2,1537,128]{2,0,1:T(2,128)(2,1)}, bf16[2,1537,128]{2,0,1:T(2,128)(2,1)S(1)}, u32[]{:S(2)}, u32[]{:S(2)}) %collective-permute-start) | collective-permute-done | bytes 786976 | tf_op jit(solution)/shard_map/ppermute | solution.py:25
  121.6 22.8 %collective-permute-done.1 = bf16[4,1537,128]{2,0,1:T(4,128)(2,1)} collective-permute-done((bf16[4,1537,128]{2,0,1:T(4,128)(2,1)S(1)}, bf16[4,1537,128]{2,0,1:T(4,128)(2,1)}, u32[]{:S(2)}, u32[]{:S(2)}) %collective-permute-start.1) | collective-permute-done | bytes 1573920 | tf_op jit(solution)/shard_map/ppermute | solution.py:25
  147.3 31.8 %collective-permute-done.2 = bf16[4,1537,128]{2,0,1:T(4,128)(2,1)} collective-permute-done((bf16[4,1537,128]{2,0,1:T(4,128)(2,1)S(1)}, bf16[4,1537,128]{2,0,1:T(4,128)(2,1)}, u32[]{:S(2)}, u32[]{:S(2)}) %collective-permute-start.2) | collective-permute-done | bytes 1573920 | tf_op jit(solution)/shard_map/ppermute | solution.py:25
  185.2 8.2 %copy.60 = bf16[2,8,1537,128]{3,1,2,0:T(8,128)(2,1)S(1)} copy(bf16[2,8,1537,128]{3,2,1,0:T(8,128)(2,1)} %bitcast.40) | data formatting | bytes 12591104
  195.5 8.9 %reshape.103 = bf16[64,6,64,64]{3,2,1,0:T(8,128)(2,1)} reshape(bf16[16,98304]{1,0:T(8,128)(2,1)} %get-tuple-element.9) | data formatting | bytes 6291456 | tf_op jit(solution)/shard_map/reshape | solution.py:60
  204.5 15.9 %convolution_convert_fusion = bf16[64,16,64,64]{3,1,2,0:T(8,128)(2,1)} fusion(bf16[64,6,64,64]{3,2,1,0:T(8,128)(2,1)} %reshape.103, s32[64,6]{1,0:T(8,128)S(1)} %eq.36), kind=kOutput, calls=%fused_computation | convolution fusion | flops 54532096 | bytes 11535872 | tf_op jit(solution)/shard_map/csb,cskn->cbkn/dot_general | solution.py:15
  220.4 23.6 %copy.38 = bf16[64,16,64,64]{2,3,1,0:T(8,128)(2,1)} copy(bf16[64,16,64,64]{3,1,2,0:T(8,128)(2,1)} %convolution_convert_fusion) | data formatting | bytes 16777216 | tf_op jit(solution)/shard_map/convert_element_type | solution.py:16
  244.0 8.5 %reshape.102 = bf16[16,24,64,64]{3,2,1,0:T(8,128)(2,1)} reshape(bf16[16,98304]{1,0:T(8,128)(2,1)S(1)} %get-tuple-element.10) | data formatting | bytes 6291456 | tf_op jit(solution)/shard_map/reshape | solution.py:59
  252.5 11.9 %convolution_convert_fusion.1 = bf16[16,64,64,64]{3,1,2,0:T(8,128)(2,1)} fusion(bf16[16,24,64,64]{3,2,1,0:T(8,128)(2,1)} %reshape.102, s32[16,24]{1,0:T(8,128)S(1)} %get-tuple-element.14), kind=kOutput, calls=%fused_computation.1 | convolution fusion | flops 205545472 | bytes 11535872 | tf_op jit(solution)/shard_map/csb,cskn->cbkn/dot_general | solution.py:15
  264.4 23.2 %copy.36 = bf16[16,64,64,64]{2,3,1,0:T(8,128)(2,1)} copy(bf16[16,64,64,64]{3,1,2,0:T(8,128)(2,1)} %convolution_convert_fusion.1) | data formatting | bytes 16777216 | tf_op jit(solution)/shard_map/convert_element_type | solution.py:16
  287.7 6.5 %copy.27 = bf16[512,4096]{0,1:T(8,128)(2,1)} copy(bf16[512,4096]{1,0:T(8,128)(2,1)} %all-gather.7.cloned.1.call-done) | data formatting | bytes 8388608 | tf_op jit(solution)/shard_map/all_gather | solution.py:75
  294.1 10.2 %fusion.19 = bf16[512,16,64,1]{0,2,1,3:T(8,128)(2,1)S(1)} fusion(bf16[512,64,64,1]{0,2,1,3:T(8,128)(2,1)} %bitcast.82, bf16[16,64,64,64]{2,3,1,0:T(8,128)(2,1)} %copy.36), kind=kOutput, calls=%fused_computation.33 | convolution fusion | flops 4299685888 | bytes 13631488 | tf_op jit(solution)/shard_map/tbk,cbkn->tcn/dot_general | solution.py:78
  304.3 10.3 %bitcast_convert_fusion.1 = bf16[512,64,64]{0,2,1:T(8,128)(2,1)} fusion(bf16[512,16,64,1]{0,2,1,3:T(8,128)(2,1)S(1)} %fusion.19, bf16[64,16,64,64]{2,3,1,0:T(8,128)(2,1)} %copy.38), kind=kOutput, calls=%fused_computation.3 | convolution fusion | flops 4297064448 | bytes 13631488 | tf_op jit(solution)/shard_map/thi,jhin->tjn/dot_general | solution.py:80
  314.6 6.5 %copy.39 = bf16[512,4096]{1,0:T(8,128)(2,1)} copy(bf16[512,4096]{0,1:T(8,128)(2,1)} %bitcast.83) | data formatting | bytes 8388608 | tf_op jit(solution)/shard_map/convert_element_type | solution.py:84
  321.2 6.7 %copy.40 = bf16[512,4096]{0,1:T(8,128)(2,1)} copy(bf16[512,4096]{1,0:T(8,128)(2,1)} %all-gather.11.cloned.1.call-done) | data formatting | bytes 8388608 | tf_op jit(solution)/shard_map/all_gather | solution.py:75
  327.9 10.2 %fusion.18 = bf16[512,16,64,1]{0,2,1,3:T(8,128)(2,1)S(1)} fusion(bf16[512,64,64,1]{0,2,1,3:T(8,128)(2,1)} %bitcast.80, bf16[16,64,64,64]{2,3,1,0:T(8,128)(2,1)} %copy.36), kind=kOutput, calls=%fused_computation.32 | convolution fusion | flops 4299685888 | bytes 13631488 | tf_op jit(solution)/shard_map/tbk,cbkn->tcn/dot_general | solution.py:78
  338.1 10.5 %bitcast_convert_fusion = bf16[512,64,64]{0,2,1:T(8,128)(2,1)} fusion(bf16[512,16,64,1]{0,2,1,3:T(8,128)(2,1)S(1)} %fusion.18, bf16[64,16,64,64]{2,3,1,0:T(8,128)(2,1)} %copy.38), kind=kOutput, calls=%fused_computation.2 | convolution fusion | flops 4297064448 | bytes 13631488 | tf_op jit(solution)/shard_map/thi,jhin->tjn/dot_general | solution.py:80
  355.0 24.7 %reduce-scatter.5.cloned.1.call-done = bf16[128,4096]{1,0:T(8,128)(2,1)} async-done(((bf16[512,4096]{1,0:T(8,128)(2,1)}), bf16[128,4096]{1,0:T(8,128)(2,1)}) %reduce-scatter.5.cloned.1.call-update) | async-done | bytes 1048592 | tf_op jit(solution)/shard_map/reduce_scatter | solution.py:83
  379.8 51.5 %reduce-scatter.9.cloned.1.call-done = bf16[128,4096]{1,0:T(8,128)(2,1)} async-done(((bf16[512,4096]{1,0:T(8,128)(2,1)}), bf16[128,4096]{1,0:T(8,128)(2,1)}) %reduce-scatter.9.cloned.1.call-update) | async-done | bytes 1048592 | tf_op jit(solution)/shard_map/reduce_scatter | solution.py:83
  431.3 34.5 %reduce-scatter.7.cloned.1.call-done = bf16[32,4096]{1,0:T(8,128)(2,1)} async-done(((bf16[128,4096]{1,0:T(8,128)(2,1)}), bf16[32,4096]{1,0:T(8,128)(2,1)}) %reduce-scatter.7.cloned.1.call-update) | async-done | bytes 262160 | tf_op jit(solution)/shard_map/reduce_scatter | solution.py:86
  465.9 34.0 %reduce-scatter.11.cloned.1.call-done = bf16[32,4096]{1,0:T(8,128)(2,1)} async-done(((bf16[128,4096]{1,0:T(8,128)(2,1)}), bf16[32,4096]{1,0:T(8,128)(2,1)}) %reduce-scatter.11.cloned.1.call-update) | async-done | bytes 262160 | tf_op jit(solution)/shard_map/reduce_scatter | solution.py:86
  (56 shorter events, 48.0 us)
Async XLA Ops:
  6.5 46.0 %all-gather.5.cloned.1.call-start = ((), (), s32[]{:S(2)}) async-start(), calls=%async_computation.4 | async-start | bytes 1310720 | tf_op jit(solution)/shard_map/all_gather | solution.py:74
  15.8 105.8 %all-gather.9.cloned.1.call-start = ((), (), s32[]{:S(2)}) async-start(), calls=%async_computation.8 | async-start | bytes 1310720 | tf_op jit(solution)/shard_map/all_gather | solution.py:74
  16.6 271.1 %all-gather.7.cloned.1.call-start = ((), (), s32[]{:S(2)}) async-start(), calls=%async_computation.5 | async-start | bytes 5242880 | tf_op jit(solution)/shard_map/all_gather | solution.py:75
  52.5 268.6 %all-gather.11.cloned.1.call-start = ((), (), s32[]{:S(2)}) async-start(), calls=%async_computation.9 | async-start | bytes 5242880 | tf_op jit(solution)/shard_map/all_gather | solution.py:75
  62.5 47.6 %collective-permute-start = (bf16[2,1537,128]{2,0,1:T(2,128)(2,1)}, bf16[2,1537,128]{2,0,1:T(2,128)(2,1)S(1)}, u32[]{:S(2)}, u32[]{:S(2)}) collective-permute-start(bf16[2,1537,128]{2,0,1:T(2,128)(2,1)} %copy.29), channel_id=1, source_target_pairs={{0,32},{32,0},{1,33},{33,1},{2,34},{34,2},{3,35},{35,3},{4,36},{36... | collective-permute-start | bytes 2360840 | tf_op jit(solution)/shard_map/ppermute | solution.py:25
  111.4 33.1 %collective-permute-start.1 = (bf16[4,1537,128]{2,0,1:T(4,128)(2,1)S(1)}, bf16[4,1537,128]{2,0,1:T(4,128)(2,1)}, u32[]{:S(2)}, u32[]{:S(2)}) collective-permute-start(bf16[4,1537,128]{2,0,1:T(4,128)(2,1)S(1)} %bitcast.77), channel_id=1, source_target_pairs={{0,64},{64,128},{128,192},{192,0},{1,65},{65,129},{129,193},{193,1... | collective-permute-start | bytes 4721672 | tf_op jit(solution)/shard_map/ppermute | solution.py:25
  112.5 66.5 %collective-permute-start.2 = (bf16[4,1537,128]{2,0,1:T(4,128)(2,1)S(1)}, bf16[4,1537,128]{2,0,1:T(4,128)(2,1)}, u32[]{:S(2)}, u32[]{:S(2)}) collective-permute-start(bf16[4,1537,128]{2,0,1:T(4,128)(2,1)S(1)} %bitcast.78), channel_id=1, source_target_pairs={{0,128},{64,192},{128,0},{192,64},{1,129},{65,193},{129,1},{193,65... | collective-permute-start | bytes 4721672 | tf_op jit(solution)/shard_map/ppermute | solution.py:25
  115.0 67.3 %collective-permute-start.3 = (bf16[4,1537,128]{2,0,1:T(4,128)(2,1)S(1)}, bf16[4,1537,128]{2,0,1:T(4,128)(2,1)}, u32[]{:S(2)}, u32[]{:S(2)}) collective-permute-start(bf16[4,1537,128]{2,0,1:T(4,128)(2,1)S(1)} %bitcast.79), channel_id=1, source_target_pairs={{0,192},{64,0},{128,64},{192,128},{1,193},{65,1},{129,65},{193,129... | collective-permute-start | bytes 4721672 | tf_op jit(solution)/shard_map/ppermute | solution.py:25
  121.6 258.1 %reduce-scatter.5.cloned.1.call-start = ((), (), s32[]{:S(2)}) async-start(), calls=%async_computation.6 | async-start | bytes 5242880 | tf_op jit(solution)/shard_map/reduce_scatter | solution.py:83
  321.1 110.2 %reduce-scatter.9.cloned.1.call-start = ((), (), s32[]{:S(2)}) async-start(), calls=%async_computation.10 | async-start | bytes 5242880 | tf_op jit(solution)/shard_map/reduce_scatter | solution.py:83
  355.0 145.0 %copy-start = (bf16[64,4096]{1,0:T(8,128)(2,1)S(1)}, bf16[64,4096]{1,0:T(8,128)(2,1)}, u32[]{:S(2)}) copy-start(bf16[64,4096]{1,0:T(8,128)(2,1)} %param.8) | copy-start | bytes 1572868
  355.0 110.9 %reduce-scatter.7.cloned.1.call-start = ((), (), s32[]{:S(2)}) async-start(), calls=%async_computation.7 | async-start | bytes 1310720 | tf_op jit(solution)/shard_map/reduce_scatter | solution.py:86
  379.7 120.2 %reduce-scatter.11.cloned.1.call-start = ((), (), s32[]{:S(2)}) async-start(), calls=%async_computation.11 | async-start | bytes 1310720 | tf_op jit(solution)/shard_map/reduce_scatter | solution.py:86
Sparse Core Ops, SparseCore 0:
  15.9 36.5 all-gather.4
  54.3 57.7 all-gather.8
  114.0 53.5 all-gather.6
  169.3 51.0 all-gather.10
  321.2 58.4 reduce-scatter.4
  382.1 49.1 reduce-scatter.8
  433.8 31.9 reduce-scatter.6
  468.4 31.4 reduce-scatter.10

commit v5 on v3

--- a/solution.py
+++ b/solution.py
@@ -50,6 +50,7 @@
     packed = jnp.concatenate(
         [up_w.reshape(-1), down_w.reshape(-1), ints, jnp.zeros((pad,), jnp.bfloat16)]
     ).reshape(1, -1, LANES)
+    normed, packed = lax.optimization_barrier((normed, packed))
     gathered_w = lax.all_gather(packed, "core", axis=0, tiled=True)
     gathered_w = permute_gather(gathered_w, "zhi")
     gathered_w = permute_gather(gathered_w, "y")

time: 461 us -> 464 us (level)
  transfers between devices with their start and end apart: 8 -> 8, of which waited for: 7 -> 7; matrix products, arithmetic and copies ran while one was open for 16% -> 15% of each run, Pallas kernels for 0% -> 0%
where the time goes in v5:
time: 464 us; the launch traced here: 455 us
  waiting for transfers between devices  264 us (57%)
  matrix products  76.2 us (16%)
  local copies, waits for them, and re-layouts  74.9 us (16%)
  between operations  14.4 us (3%)
  starting transfers between devices  10.7 us (2%)
  other arithmetic  10.2 us (2%)
  blocking collectives  5.19 us (1%)
    reduce_scatter x1, waiting for transfers between devices, on_device(): lax.psum_scatter(partial_sums.astype(jnp.bfloat16), 'x', scatter_dimensio...  84.3 us
    ppermute x4, waiting for transfers between devices, permute_gather(): lax.ppermute(piece, axis, [(i, (i + shift) % size) for i in range(size)])  74.7 us
    all_gather x1, waiting for transfers between devices, on_device(): gathered = lax.all_gather(gathered, 'x', axis=0, tiled=True)  53.8 us
    reduce_scatter x1, waiting for transfers between devices, on_device(): lax.psum_scatter(summed, 'zlo', scatter_dimension=0, tiled=True)  50.7 us
    dot_general x1, matrix products, on_device(): jnp.einsum('tbk,cbkn->tcn', row_blocks, dense_up, preferred_element_type=...  31.9 us
    dot_general x2, matrix products, onehot_dense(): jnp.einsum('csb,cskn->cbkn', onehot, weights, preferred_element_type=jnp....  25.6 us
    dot_general x1, matrix products, on_device(): jnp.einsum('thi,jhin->tjn', hidden, dense_down, preferred_element_type=jn...  18.7 us
    all_gather x1, local copies, waits for them, and re-layouts, on_device(): gathered = lax.all_gather(gathered, 'x', axis=0, tiled=True)  11.9 us
  transfers between devices with their start and end apart: 8, of which 7 were waited for; matrix products, arithmetic and copies ran while one was open for 15% of the time, Pallas kernels for 0%

profile of v5, /device:TPU:1, one launch (start us, length us, event | category | flops | bytes accessed | tf_op | source)
XLA Modules:
  0.0 455.1 jit_solution(13253931921679590302)
XLA Ops:
  13.2 2.0 fusion.21
  15.7 5.2 %all_gather.11 = bf16[2,1537,128]{2,1,0:T(8,128)(2,1)S(1)} all-gather(bf16[1,1537,128]{2,1,0:T(8,128)(2,1)S(1)} %bitcast.61), channel_id=1, replica_groups=mesh['y'=4,'zhi'=2,'core'=2,'x'=4,'zlo'=4] {'core'}, dimensions={0}, use_global_device_ids=true | all-gather | bytes 1180416 | tf_op jit(solution)/shard_map/all_gather | solution.py:54
  20.9 6.4 %copy.26 = bf16[2,1537,128]{2,0,1:T(2,128)(2,1)} copy(bf16[2,1537,128]{2,1,0:T(8,128)(2,1)S(1)} %all_gather.11) | data formatting | bytes 1573888 | tf_op jit(solution)/shard_map/all_gather | solution.py:54
  27.3 5.2 %collective-permute-start = (bf16[2,1537,128]{2,0,1:T(2,128)(2,1)}, bf16[2,1537,128]{2,0,1:T(2,128)(2,1)S(1)}, u32[]{:S(2)}, u32[]{:S(2)}) collective-permute-start(bf16[2,1537,128]{2,0,1:T(2,128)(2,1)} %copy.26), channel_id=1, source_target_pairs={{0,32},{32,0},{1,33},{33,1},{2,34},{34,2},{3,35},{35,3},{4,36},{36... | collective-permute-start | bytes 2360840 | tf_op jit(solution)/shard_map/ppermute | solution.py:25
  33.4 6.4 %copy_dynamic-update-slice_fusion.3 = bf16[2,2,1537,128]{3,1,0,2:T(2,128)(2,1)S(1)} fusion(bf16[2,2,1537,128]{3,1,0,2:T(2,128)(2,1)S(1)} %broadcast_in_dim.42, s32[]{:T(128)S(6)} %select_n.39, bf16[1,2,1537,128]{3,2,1,0:T(8,128)(2,1)S(1)} %bitcast.56), kind=kLoop, calls=%fused_computation.32 | loop fusion | bytes 1577476 | tf_op jit(solution)/shard_map/jit(dynamic_update_index_in_dim)/dynamic_update_slice | solution.py:23
  39.8 13.7 %collective-permute-done = bf16[2,1537,128]{2,0,1:T(2,128)(2,1)S(1)} collective-permute-done((bf16[2,1537,128]{2,0,1:T(2,128)(2,1)}, bf16[2,1537,128]{2,0,1:T(2,128)(2,1)S(1)}, u32[]{:S(2)}, u32[]{:S(2)}) %collective-permute-start) | collective-permute-done | bytes 786976 | tf_op jit(solution)/shard_map/ppermute | solution.py:25
  56.4 2.7 collective-permute-start.2
  61.5 17.8 %collective-permute-done.1 = bf16[4,1537,128]{2,0,1:T(4,128)(2,1)} collective-permute-done((bf16[4,1537,128]{2,0,1:T(4,128)(2,1)S(1)}, bf16[4,1537,128]{2,0,1:T(4,128)(2,1)}, u32[]{:S(2)}, u32[]{:S(2)}) %collective-permute-start.1) | collective-permute-done | bytes 1573920 | tf_op jit(solution)/shard_map/ppermute | solution.py:25
  81.1 32.8 %collective-permute-done.2 = bf16[4,1537,128]{2,0,1:T(4,128)(2,1)} collective-permute-done((bf16[4,1537,128]{2,0,1:T(4,128)(2,1)S(1)}, bf16[4,1537,128]{2,0,1:T(4,128)(2,1)}, u32[]{:S(2)}, u32[]{:S(2)}) %collective-permute-start.2) | collective-permute-done | bytes 1573920 | tf_op jit(solution)/shard_map/ppermute | solution.py:25
  115.8 10.3 %collective-permute-done.3 = bf16[4,1537,128]{2,0,1:T(4,128)(2,1)} collective-permute-done((bf16[4,1537,128]{2,0,1:T(4,128)(2,1)S(1)}, bf16[4,1537,128]{2,0,1:T(4,128)(2,1)}, u32[]{:S(2)}, u32[]{:S(2)}) %collective-permute-start.3) | collective-permute-done | bytes 1573920 | tf_op jit(solution)/shard_map/ppermute | solution.py:25
  127.8 7.1 %copy.59 = bf16[2,8,1537,128]{3,1,2,0:T(8,128)(2,1)} copy(bf16[2,8,1537,128]{3,2,1,0:T(8,128)(2,1)S(1)} %bitcast.51) | data formatting | bytes 12591104
  135.0 4.9 %fusion.30 = (bf16[16,98304]{1,0:T(8,128)(2,1)}, bf16[16,98304]{1,0:T(8,128)(2,1)S(1)}) fusion(bf16[16,196736]{1,0:T(8,128)(2,1)} %bitcast.52), kind=kLoop, calls=%fused_computation.47 | loop fusion | bytes 12582912 | tf_op jit(solution)/shard_map/slice | solution.py:59
  139.9 8.8 %reshape.97 = bf16[16,24,64,64]{3,2,1,0:T(8,128)(2,1)} reshape(bf16[16,98304]{1,0:T(8,128)(2,1)} %get-tuple-element.9) | data formatting | bytes 6291456 | tf_op jit(solution)/shard_map/reshape | solution.py:59
  148.7 8.3 %reshape.98 = bf16[64,6,64,64]{3,2,1,0:T(8,128)(2,1)} reshape(bf16[16,98304]{1,0:T(8,128)(2,1)S(1)} %get-tuple-element.10) | data formatting | bytes 6291456 | tf_op jit(solution)/shard_map/reshape | solution.py:60
  157.9 12.8 %convolution_convert_fusion.1 = bf16[16,64,64,64]{3,1,2,0:T(8,128)(2,1)} fusion(bf16[16,24,64,64]{3,2,1,0:T(8,128)(2,1)} %reshape.97, s32[16,24]{1,0:T(8,128)S(1)} %get-tuple-element.11), kind=kOutput, calls=%fused_computation.6 | convolution fusion | flops 205545472 | bytes 11535872 | tf_op jit(solution)/shard_map/csb,cskn->cbkn/dot_general | solution.py:15
  170.7 12.8 %convolution_convert_fusion = bf16[64,16,64,64]{3,1,2,0:T(8,128)(2,1)} fusion(bf16[64,6,64,64]{3,2,1,0:T(8,128)(2,1)S(1)} %copy-done, s32[64,6]{1,0:T(8,128)S(1)} %eq.36), kind=kOutput, calls=%fused_computation.5 | convolution fusion | flops 54532096 | bytes 11535872 | tf_op jit(solution)/shard_map/csb,cskn->cbkn/dot_general | solution.py:15
  183.5 53.8 %all-gather.5.cloned.1.call-done = bf16[1024,4096]{1,0:T(8,128)(2,1)} async-done(((bf16[256,4096]{1,0:T(8,128)(2,1)}), bf16[1024,4096]{1,0:T(8,128)(2,1)}) %all-gather.5.cloned.1.call-update) | async-done | bytes 8388624 | tf_op jit(solution)/shard_map/all_gather | solution.py:66
  237.3 11.9 %copy.24 = bf16[1024,4096]{0,1:T(8,128)(2,1)} copy(bf16[1024,4096]{1,0:T(8,128)(2,1)} %all-gather.5.cloned.1.call-done) | data formatting | bytes 16777216 | tf_op jit(solution)/shard_map/all_gather | solution.py:66
  249.2 31.9 %fusion.15 = bf16[1024,16,64]{0,2,1:T(8,128)(2,1)S(1)} fusion(bf16[1024,64,64,1]{0,2,1,3:T(8,128)(2,1)} %bitcast.54, bf16[16,64,64,64]{3,1,2,0:T(8,128)(2,1)} %convolution_convert_fusion.1), kind=kOutput, calls=%fused_computation.18 | convolution fusion | flops 8599371776 | bytes 18874368 | tf_op jit(solution)/shard_map/tbk,cbkn->tcn/dot_general | solution.py:71
  281.2 18.7 %bitcast_convert_fusion = bf16[1024,64,64]{0,2,1:T(8,128)(2,1)} fusion(bf16[64,16,64,64]{3,1,2,0:T(8,128)(2,1)} %convolution_convert_fusion, bf16[1024,16,64]{0,2,1:T(8,128)(2,1)S(1)} %fusion.15), kind=kOutput, calls=%fused_computation | convolution fusion | flops 8594128896 | bytes 18874368 | tf_op jit(solution)/shard_map/thi,jhin->tjn/dot_general | solution.py:76
  299.9 11.2 %copy.36 = bf16[1024,4096]{1,0:T(8,128)(2,1)} copy(bf16[1024,4096]{0,1:T(8,128)(2,1)} %bitcast.55) | data formatting | bytes 16777216 | tf_op jit(solution)/shard_map/convert_element_type | solution.py:80
  311.2 84.3 %reduce-scatter.3.cloned.1.call-done = bf16[256,4096]{1,0:T(8,128)(2,1)} async-done(((bf16[1024,4096]{1,0:T(8,128)(2,1)}), bf16[256,4096]{1,0:T(8,128)(2,1)}) %reduce-scatter.3.cloned.1.call-update) | async-done | bytes 2097168 | tf_op jit(solution)/shard_map/reduce_scatter | solution.py:79
  395.5 50.7 %reduce-scatter.5.cloned.1.call-done = bf16[64,4096]{1,0:T(8,128)(2,1)} async-done(((bf16[256,4096]{1,0:T(8,128)(2,1)}), bf16[64,4096]{1,0:T(8,128)(2,1)}) %reduce-scatter.5.cloned.1.call-update) | async-done | bytes 524304 | tf_op jit(solution)/shard_map/reduce_scatter | solution.py:82
  446.2 2.0 fusion.22
  (39 shorter events, 18.8 us)
Async XLA Ops:
  6.5 128.4 %all-gather.3.cloned.1.call-start = ((), (), s32[]{:S(2)}) async-start(), calls=%async_computation.2 | async-start | bytes 2621440 | tf_op jit(solution)/shard_map/all_gather | solution.py:65
  27.3 26.2 %collective-permute-start = (bf16[2,1537,128]{2,0,1:T(2,128)(2,1)}, bf16[2,1537,128]{2,0,1:T(2,128)(2,1)S(1)}, u32[]{:S(2)}, u32[]{:S(2)}) collective-permute-start(bf16[2,1537,128]{2,0,1:T(2,128)(2,1)} %copy.26), channel_id=1, source_target_pairs={{0,32},{32,0},{1,33},{33,1},{2,34},{34,2},{3,35},{35,3},{4,36},{36... | collective-permute-start | bytes 2360840 | tf_op jit(solution)/shard_map/ppermute | solution.py:25
  54.8 24.5 %collective-permute-start.1 = (bf16[4,1537,128]{2,0,1:T(4,128)(2,1)S(1)}, bf16[4,1537,128]{2,0,1:T(4,128)(2,1)}, u32[]{:S(2)}, u32[]{:S(2)}) collective-permute-start(bf16[4,1537,128]{2,0,1:T(4,128)(2,1)S(1)} %bitcast.58), channel_id=1, source_target_pairs={{0,64},{64,128},{128,192},{192,0},{1,65},{65,129},{129,193},{193,1... | collective-permute-start | bytes 4721672 | tf_op jit(solution)/shard_map/ppermute | solution.py:25
  56.3 181.0 %all-gather.5.cloned.1.call-start = ((), (), s32[]{:S(2)}) async-start(), calls=%async_computation.3 | async-start | bytes 10485760 | tf_op jit(solution)/shard_map/all_gather | solution.py:66
  56.4 57.6 %collective-permute-start.2 = (bf16[4,1537,128]{2,0,1:T(4,128)(2,1)S(1)}, bf16[4,1537,128]{2,0,1:T(4,128)(2,1)}, u32[]{:S(2)}, u32[]{:S(2)}) collective-permute-start(bf16[4,1537,128]{2,0,1:T(4,128)(2,1)S(1)} %bitcast.59), channel_id=1, source_target_pairs={{0,128},{64,192},{128,0},{192,64},{1,129},{65,193},{129,1},{193,65... | collective-permute-start | bytes 4721672 | tf_op jit(solution)/shard_map/ppermute | solution.py:25
  59.1 67.0 %collective-permute-start.3 = (bf16[4,1537,128]{2,0,1:T(4,128)(2,1)S(1)}, bf16[4,1537,128]{2,0,1:T(4,128)(2,1)}, u32[]{:S(2)}, u32[]{:S(2)}) collective-permute-start(bf16[4,1537,128]{2,0,1:T(4,128)(2,1)S(1)} %bitcast.60), channel_id=1, source_target_pairs={{0,192},{64,0},{128,64},{192,128},{1,193},{65,1},{129,65},{193,129... | collective-permute-start | bytes 4721672 | tf_op jit(solution)/shard_map/ppermute | solution.py:25
  135.0 260.5 %reduce-scatter.3.cloned.1.call-start = ((), (), s32[]{:S(2)}) async-start(), calls=%async_computation.4 | async-start | bytes 10485760 | tf_op jit(solution)/shard_map/reduce_scatter | solution.py:79
  157.9 12.8 %copy-start = (bf16[64,6,64,64]{3,2,1,0:T(8,128)(2,1)S(1)}, bf16[64,6,64,64]{3,2,1,0:T(8,128)(2,1)}, u32[]{:S(2)}) copy-start(bf16[64,6,64,64]{3,2,1,0:T(8,128)(2,1)} %reshape.98) | copy-start | bytes 9437188
  311.1 135.1 %copy-start.1 = (bf16[64,4096]{1,0:T(8,128)(2,1)S(1)}, bf16[64,4096]{1,0:T(8,128)(2,1)}, u32[]{:S(2)}) copy-start(bf16[64,4096]{1,0:T(8,128)(2,1)} %param.8) | copy-start | bytes 1572868
  311.1 135.1 %reduce-scatter.5.cloned.1.call-start = ((), (), s32[]{:S(2)}) async-start(), calls=%async_computation.5 | async-start | bytes 2621440 | tf_op jit(solution)/shard_map/reduce_scatter | solution.py:82
Sparse Core Ops, SparseCore 0:
  56.4 64.2 all-gather.2
  135.1 102.1 all-gather.4
  311.2 84.1 reduce-scatter.2
  397.8 48.2 reduce-scatter.4

commit v6 on v3

--- a/solution.py
+++ b/solution.py
@@ -25,6 +25,18 @@
         moved = lax.ppermute(piece, axis, [(i, (i + shift) % size) for i in range(size)])
         whole = lax.dynamic_update_index_in_dim(whole, moved, (me - shift) % size, 0)
     return whole.reshape((size * piece.shape[0],) + piece.shape[1:])
+
+
+def permute_reduce_scatter(whole, axis):
+    size = lax.axis_size(axis)
+    me = lax.axis_index(axis)
+    chunks = whole.reshape((size, whole.shape[0] // size) + whole.shape[1:])
+    acc = lax.dynamic_index_in_dim(chunks, me, 0, keepdims=False).astype(jnp.float32)
+    for shift in range(1, size):
+        send = lax.dynamic_index_in_dim(chunks, (me + shift) % size, 0, keepdims=False)
+        moved = lax.ppermute(send, axis, [(i, (i + shift) % size) for i in range(size)])
+        acc = acc + moved.astype(jnp.float32)
+    return acc
 
 
 def on_device(tokens, norm_gain, up_blocks, up_rows, up_count, down_blocks, down_rows, down_count):
@@ -78,7 +90,7 @@
     summed = lax.psum_scatter(
         partial_sums.astype(jnp.bfloat16), "x", scatter_dimension=0, tiled=True
     )
-    summed = lax.psum_scatter(summed, "zlo", scatter_dimension=0, tiled=True).astype(jnp.float32)
+    summed = permute_reduce_scatter(summed, "zlo")
     return (x_float + summed).astype(jnp.bfloat16)
 
 

time: 461 us -> 451 us (0.978)
  the two profiles are of different devices: /device:TPU:1 before, /device:TPU:33 now
where the time goes in v6:
time: 451 us; the launch traced here: 443 us
  waiting for transfers between devices  258 us (57%)
  matrix products  75.7 us (17%)
  local copies, waits for them, and re-layouts  68.8 us (15%)
  starting transfers between devices  15.1 us (3%)
  between operations  14.2 us (3%)
  other arithmetic  8.62 us (2%)
    ppermute x4, waiting for transfers between devices, permute_gather(): lax.ppermute(piece, axis, [(i, (i + shift) % size) for i in range(size)])  89 us
    reduce_scatter x1, waiting for transfers between devices, on_device(): lax.psum_scatter(partial_sums.astype(jnp.bfloat16), 'x', scatter_dimensio...  84.3 us
    ppermute x3, waiting for transfers between devices, permute_reduce_scatter(): lax.ppermute(send, axis, [(i, (i + shift) % size) for i in range(size)])  45 us
    all_gather x1, waiting for transfers between devices, on_device(): gathered = lax.all_gather(gathered, 'x', axis=0, tiled=True)  39.6 us
    dot_general x1, matrix products, on_device(): jnp.einsum('tbk,cbkn->tcn', row_blocks, dense_up, preferred_element_type=...  32 us
    dot_general x2, matrix products, onehot_dense(): jnp.einsum('csb,cskn->cbkn', onehot, weights, preferred_element_type=jnp....  24.9 us
    dot_general x1, matrix products, on_device(): jnp.einsum('thi,jhin->tjn', hidden, dense_down, preferred_element_type=jn...  18.7 us
    all_gather x1, local copies, waits for them, and re-layouts, on_device(): gathered = lax.all_gather(gathered, 'x', axis=0, tiled=True)  11.9 us
  transfers between devices with their start and end apart: 10, of which 8 were waited for; matrix products, arithmetic and copies ran while one was open for 16% of the time, Pallas kernels for 0%

profile of v6, /device:TPU:33, one launch (start us, length us, event | category | flops | bytes accessed | tf_op | source)
XLA Modules:
  0.0 443.0 jit_solution(1773715758021496308)
XLA Ops:
  12.5 2.7 all_gather.11
  15.1 6.4 %copy.26 = bf16[2,1537,128]{2,0,1:T(2,128)(2,1)} copy(bf16[2,1537,128]{2,1,0:T(8,128)(2,1)S(1)} %all_gather.11) | data formatting | bytes 1573888 | tf_op jit(solution)/shard_map/all_gather | solution.py:65
  21.6 6.0 %collective-permute-start = (bf16[2,1537,128]{2,0,1:T(2,128)(2,1)}, bf16[2,1537,128]{2,0,1:T(2,128)(2,1)}, u32[]{:S(2)}, u32[]{:S(2)}) collective-permute-start(bf16[2,1537,128]{2,0,1:T(2,128)(2,1)} %copy.26), channel_id=1, source_target_pairs={{0,32},{32,0},{1,33},{33,1},{2,34},{34,2},{3,35},{35,3},{4,36},{36... | collective-permute-start | bytes 2360840 | tf_op jit(solution)/shard_map/ppermute | solution.py:25
  28.7 6.4 %copy_dynamic-update-slice_fusion.3 = bf16[2,2,1537,128]{3,1,0,2:T(2,128)(2,1)S(1)} fusion(bf16[2,2,1537,128]{3,1,0,2:T(2,128)(2,1)S(1)} %broadcast_in_dim.41, s32[]{:T(128)S(6)} %select_n.64, bf16[1,2,1537,128]{3,2,1,0:T(8,128)(2,1)S(1)} %bitcast.68), kind=kLoop, calls=%fused_computation.35 | loop fusion | bytes 1577476 | tf_op jit(solution)/shard_map/jit(dynamic_update_index_in_dim)/dynamic_update_slice | solution.py:23
  35.1 27.2 %collective-permute-done = bf16[2,1537,128]{2,0,1:T(2,128)(2,1)} collective-permute-done((bf16[2,1537,128]{2,0,1:T(2,128)(2,1)}, bf16[2,1537,128]{2,0,1:T(2,128)(2,1)}, u32[]{:S(2)}, u32[]{:S(2)}) %collective-permute-start) | collective-permute-done | bytes 786976 | tf_op jit(solution)/shard_map/ppermute | solution.py:25
  67.0 2.7 collective-permute-start.2
  72.2 28.8 %collective-permute-done.1 = bf16[4,1537,128]{2,0,1:T(4,128)(2,1)} collective-permute-done((bf16[4,1537,128]{2,0,1:T(4,128)(2,1)S(1)}, bf16[4,1537,128]{2,0,1:T(4,128)(2,1)}, u32[]{:S(2)}, u32[]{:S(2)}) %collective-permute-start.1) | collective-permute-done | bytes 1573920 | tf_op jit(solution)/shard_map/ppermute | solution.py:25
  102.8 33.0 %collective-permute-done.2 = bf16[4,1537,128]{2,0,1:T(4,128)(2,1)} collective-permute-done((bf16[4,1537,128]{2,0,1:T(4,128)(2,1)S(1)}, bf16[4,1537,128]{2,0,1:T(4,128)(2,1)}, u32[]{:S(2)}, u32[]{:S(2)}) %collective-permute-start.2) | collective-permute-done | bytes 1573920 | tf_op jit(solution)/shard_map/ppermute | solution.py:25
  139.4 7.1 %copy.59 = bf16[2,8,1537,128]{3,1,2,0:T(8,128)(2,1)} copy(bf16[2,8,1537,128]{3,2,1,0:T(8,128)(2,1)S(1)} %bitcast.61) | data formatting | bytes 12591104
  146.6 4.9 %fusion.32 = (bf16[16,98304]{1,0:T(8,128)(2,1)}, bf16[16,98304]{1,0:T(8,128)(2,1)S(1)}) fusion(bf16[16,196736]{1,0:T(8,128)(2,1)} %bitcast.62), kind=kLoop, calls=%fused_computation.53 | loop fusion | bytes 12582912 | tf_op jit(solution)/shard_map/slice | solution.py:70
  151.5 8.8 %reshape.102 = bf16[16,24,64,64]{3,2,1,0:T(8,128)(2,1)} reshape(bf16[16,98304]{1,0:T(8,128)(2,1)} %get-tuple-element.5) | data formatting | bytes 6291456 | tf_op jit(solution)/shard_map/reshape | solution.py:70
  160.3 8.3 %reshape.103 = bf16[64,6,64,64]{3,2,1,0:T(8,128)(2,1)} reshape(bf16[16,98304]{1,0:T(8,128)(2,1)S(1)} %get-tuple-element.6) | data formatting | bytes 6291456 | tf_op jit(solution)/shard_map/reshape | solution.py:71
  169.5 12.1 %convolution_convert_fusion.1 = bf16[16,64,64,64]{3,1,2,0:T(8,128)(2,1)} fusion(bf16[16,24,64,64]{3,2,1,0:T(8,128)(2,1)} %reshape.102, s32[16,24]{1,0:T(8,128)S(1)} %get-tuple-element.10), kind=kOutput, calls=%fused_computation.6 | convolution fusion | flops 205545472 | bytes 11535872 | tf_op jit(solution)/shard_map/csb,cskn->cbkn/dot_general | solution.py:15
  181.6 12.8 %convolution_convert_fusion = bf16[64,16,64,64]{3,1,2,0:T(8,128)(2,1)} fusion(bf16[64,6,64,64]{3,2,1,0:T(8,128)(2,1)S(1)} %copy-done, s32[64,6]{1,0:T(8,128)S(1)} %eq.39), kind=kOutput, calls=%fused_computation.5 | convolution fusion | flops 54532096 | bytes 11535872 | tf_op jit(solution)/shard_map/csb,cskn->cbkn/dot_general | solution.py:15
  194.4 39.6 %all-gather.5.cloned.1.call-done = bf16[1024,4096]{1,0:T(8,128)(2,1)} async-done(((bf16[256,4096]{1,0:T(8,128)(2,1)}), bf16[1024,4096]{1,0:T(8,128)(2,1)}) %all-gather.5.cloned.1.call-update) | async-done | bytes 8388624 | tf_op jit(solution)/shard_map/all_gather | solution.py:77
  234.0 11.9 %copy.24 = bf16[1024,4096]{0,1:T(8,128)(2,1)} copy(bf16[1024,4096]{1,0:T(8,128)(2,1)} %all-gather.5.cloned.1.call-done) | data formatting | bytes 16777216 | tf_op jit(solution)/shard_map/all_gather | solution.py:77
  246.0 32.0 %fusion.15 = bf16[1024,16,64]{0,2,1:T(8,128)(2,1)S(1)} fusion(bf16[1024,64,64,1]{0,2,1,3:T(8,128)(2,1)} %bitcast.65, bf16[16,64,64,64]{3,1,2,0:T(8,128)(2,1)} %convolution_convert_fusion.1), kind=kOutput, calls=%fused_computation.18 | convolution fusion | flops 8599371776 | bytes 18874368 | tf_op jit(solution)/shard_map/tbk,cbkn->tcn/dot_general | solution.py:82
  278.0 18.7 %bitcast_convert_fusion = bf16[1024,64,64]{0,2,1:T(8,128)(2,1)} fusion(bf16[64,16,64,64]{3,1,2,0:T(8,128)(2,1)} %convolution_convert_fusion, bf16[1024,16,64]{0,2,1:T(8,128)(2,1)S(1)} %fusion.15), kind=kOutput, calls=%fused_computation | convolution fusion | flops 8594128896 | bytes 18874368 | tf_op jit(solution)/shard_map/thi,jhin->tjn/dot_general | solution.py:87
  296.8 84.3 %reduce-scatter.2.cloned.1.call-done = bf16[256,4096]{0,1:T(8,128)(2,1)} async-done(((bf16[1024,4096]{0,1:T(8,128)(2,1)}), bf16[256,4096]{0,1:T(8,128)(2,1)}) %reduce-scatter.2.cloned.1.call-update) | async-done | bytes 2097168 | tf_op jit(solution)/shard_map/reduce_scatter | solution.py:90
  381.0 2.9 copy.36
  388.8 9.3 %collective-permute-done.4 = bf16[64,4096]{1,0:T(8,128)(2,1)} collective-permute-done((bf16[64,4096]{1,0:T(8,128)(2,1)}, bf16[64,4096]{1,0:T(8,128)(2,1)}, u32[]{:S(2)}, u32[]{:S(2)}) %collective-permute-start.4) | collective-permute-done | bytes 524320 | tf_op jit(solution)/shard_map/ppermute | solution.py:37
  398.1 32.8 %collective-permute-done.5 = bf16[64,4096]{1,0:T(8,128)(2,1)} collective-permute-done((bf16[64,4096]{1,0:T(8,128)(2,1)}, bf16[64,4096]{1,0:T(8,128)(2,1)}, u32[]{:S(2)}, u32[]{:S(2)}) %collective-permute-start.5) | collective-permute-done | bytes 524320 | tf_op jit(solution)/shard_map/ppermute | solution.py:37
  430.9 2.9 collective-permute-done.6
  433.8 2.5 fusion.22
  (47 shorter events, 24.5 us)
Async XLA Ops:
  6.5 21.0 %copy-start.1 = (bf16[64,4096]{1,0:T(8,128)(2,1)S(1)}, bf16[64,4096]{1,0:T(8,128)(2,1)}, u32[]{:S(2)}) copy-start(bf16[64,4096]{1,0:T(8,128)(2,1)} %param.8) | copy-start | bytes 1572868
  6.5 59.4 %copy-start.3 = (f32[4096]{0:T(1024)S(1)}, f32[4096]{0:T(1024)}, u32[]{:S(2)}) copy-start(f32[4096]{0:T(1024)} %param.9) | copy-start | bytes 49156
  6.5 140.0 %all-gather.3.cloned.1.call-start = ((), (), s32[]{:S(2)}) async-start(), calls=%async_computation.1 | async-start | bytes 2621440 | tf_op jit(solution)/shard_map/all_gather | solution.py:76
  21.6 40.7 %collective-permute-start = (bf16[2,1537,128]{2,0,1:T(2,128)(2,1)}, bf16[2,1537,128]{2,0,1:T(2,128)(2,1)}, u32[]{:S(2)}, u32[]{:S(2)}) collective-permute-start(bf16[2,1537,128]{2,0,1:T(2,128)(2,1)} %copy.26), channel_id=1, source_target_pairs={{0,32},{32,0},{1,33},{33,1},{2,34},{34,2},{3,35},{35,3},{4,36},{36... | collective-permute-start | bytes 2360840 | tf_op jit(solution)/shard_map/ppermute | solution.py:25
  64.6 36.4 %collective-permute-start.1 = (bf16[4,1537,128]{2,0,1:T(4,128)(2,1)S(1)}, bf16[4,1537,128]{2,0,1:T(4,128)(2,1)}, u32[]{:S(2)}, u32[]{:S(2)}) collective-permute-start(bf16[4,1537,128]{2,0,1:T(4,128)(2,1)S(1)} %bitcast.70), channel_id=1, source_target_pairs={{0,64},{64,128},{128,192},{192,0},{1,65},{65,129},{129,193},{193,1... | collective-permute-start | bytes 4721672 | tf_op jit(solution)/shard_map/ppermute | solution.py:25
  67.0 167.0 %all-gather.5.cloned.1.call-start = ((), (), s32[]{:S(2)}) async-start(), calls=%async_computation.2 | async-start | bytes 10485760 | tf_op jit(solution)/shard_map/all_gather | solution.py:77
  67.0 68.8 %collective-permute-start.2 = (bf16[4,1537,128]{2,0,1:T(4,128)(2,1)S(1)}, bf16[4,1537,128]{2,0,1:T(4,128)(2,1)}, u32[]{:S(2)}, u32[]{:S(2)}) collective-permute-start(bf16[4,1537,128]{2,0,1:T(4,128)(2,1)S(1)} %bitcast.71), channel_id=1, source_target_pairs={{0,128},{64,192},{128,0},{192,64},{1,129},{65,193},{129,1},{193,65... | collective-permute-start | bytes 4721672 | tf_op jit(solution)/shard_map/ppermute | solution.py:25
  69.7 67.9 %collective-permute-start.3 = (bf16[4,1537,128]{2,0,1:T(4,128)(2,1)S(1)}, bf16[4,1537,128]{2,0,1:T(4,128)(2,1)}, u32[]{:S(2)}, u32[]{:S(2)}) collective-permute-start(bf16[4,1537,128]{2,0,1:T(4,128)(2,1)S(1)} %bitcast.72), channel_id=1, source_target_pairs={{0,192},{64,0},{128,64},{192,128},{1,193},{65,1},{129,65},{193,129... | collective-permute-start | bytes 4721672 | tf_op jit(solution)/shard_map/ppermute | solution.py:25
  146.6 234.5 %reduce-scatter.2.cloned.1.call-start = ((), (), s32[]{:S(2)}) async-start(), calls=%async_computation.3 | async-start | bytes 10485760 | tf_op jit(solution)/shard_map/reduce_scatter | solution.py:90
  169.5 12.1 %copy-start = (bf16[64,6,64,64]{3,2,1,0:T(8,128)(2,1)S(1)}, bf16[64,6,64,64]{3,2,1,0:T(8,128)(2,1)}, u32[]{:S(2)}) copy-start(bf16[64,6,64,64]{3,2,1,0:T(8,128)(2,1)} %reshape.103) | copy-start | bytes 9437188
  296.7 137.1 %copy-start.2 = (bf16[64,4096]{1,0:T(8,128)(2,1)S(1)}, bf16[64,4096]{1,0:T(8,128)(2,1)}, u32[]{:S(2)}) copy-start(bf16[64,4096]{1,0:T(8,128)(2,1)} %param.8) | copy-start | bytes 1572868
  385.1 13.1 %collective-permute-start.4 = (bf16[64,4096]{1,0:T(8,128)(2,1)}, bf16[64,4096]{1,0:T(8,128)(2,1)}, u32[]{:S(2)}, u32[]{:S(2)}) collective-permute-start(bf16[64,4096]{1,0:T(8,128)(2,1)} %get-tuple-element.7), channel_id=1, source_target_pairs={{0,1},{1,2},{2,3},{3,0},{4,5},{5,6},{6,7},{7,4},{8,9},{9,10},{10,1... | collective-permute-start | bytes 1572872 | tf_op jit(solution)/shard_map/ppermute | solution.py:37
  386.3 44.6 %collective-permute-start.5 = (bf16[64,4096]{1,0:T(8,128)(2,1)}, bf16[64,4096]{1,0:T(8,128)(2,1)}, u32[]{:S(2)}, u32[]{:S(2)}) collective-permute-start(bf16[64,4096]{1,0:T(8,128)(2,1)} %get-tuple-element.9), channel_id=1, source_target_pairs={{0,2},{1,3},{2,0},{3,1},{4,6},{5,7},{6,4},{7,5},{8,10},{9,11},{10,... | collective-permute-start | bytes 1572872 | tf_op jit(solution)/shard_map/ppermute | solution.py:37
  387.3 46.4 %collective-permute-start.6 = (bf16[64,4096]{1,0:T(8,128)(2,1)S(1)}, bf16[64,4096]{1,0:T(8,128)(2,1)}, u32[]{:S(2)}, u32[]{:S(2)}) collective-permute-start(bf16[64,4096]{1,0:T(8,128)(2,1)S(1)} %get-tuple-element.8), channel_id=1, source_target_pairs={{0,3},{1,0},{2,1},{3,2},{4,7},{5,4},{6,5},{7,6},{8,11},{9,8},{10,9... | collective-permute-start | bytes 1572872 | tf_op jit(solution)/shard_map/ppermute | solution.py:37
Sparse Core Ops, SparseCore 0:
  67.1 50.9 all-gather.2
  146.7 87.2 all-gather.4
  296.8 84.1 reduce-scatter.1
